TPU v7x, 32 devices: a whole 2x2x4 slice. The times are simulated.
32 devices in a mesh: seq: 16 (over z, y, x), mp: 2 (over core).
Axes of the slice: x: 2, y: 2, z: 4, core: 2. Of those that a mesh axis runs over, the one named last changes fastest.
Arguments:
- layer_input: float32 [4096, 1024], P('seq'), may hold values from -6 to 6
- cotangent: float32 [4096, 1024], P('seq'), may hold values from -6 to 6
- doc_starts: int32 [4096], P('seq'), may hold values 0 or 1
- norm_gain: float32 [1024], replicated, may hold values from 0.5 to 1.5
- gate_weight: float32 [1024, 2048], P('seq', 'mp'), may hold values from -0.1875 to 0.1875
- value_weight: float32 [1024, 2048], P('seq', 'mp'), may hold values from -0.1875 to 0.1875
- state_weight: float32 [1024, 288], P('seq'), may hold values from -0.1875 to 0.1875
- conv_value: float32 [5, 2048], replicated, may hold values from -0.5 to 0.5
- conv_state: float32 [5, 256], replicated, may hold values from -0.5 to 0.5
- head_params: float32 [3, 32], replicated, as said below
- gated_gain: float32 [2048], replicated, may hold values from 0.5 to 1.5
- out_weight: float32 [1024, 2048], P('seq', 'mp'), may hold values from -0.125 to 0.125
- norm_gain_velocity: float32 [1024], replicated, may hold values from -80 to 80
- gate_weight_velocity: float32 [1024, 2048], P('seq', 'mp'), may hold values from -80 to 80
- value_weight_velocity: float32 [1024, 2048], P('seq', 'mp'), may hold values from -80 to 80
- state_weight_velocity: float32 [1024, 288], P('seq'), may hold values from -80 to 80
- conv_value_velocity: float32 [5, 2048], replicated, may hold values from -80 to 80
- conv_state_velocity: float32 [5, 256], replicated, may hold values from -80 to 80
- head_params_velocity: float32 [3, 32], replicated, may hold values from -80 to 80
- gated_gain_velocity: float32 [2048], replicated, may hold values from -80 to 80
- out_weight_velocity: float32 [1024, 2048], P('seq', 'mp'), may hold values from -80 to 80
Outputs:
- layer_output: float32 [4096, 1024], P('seq')
- input_grad: float32 [4096, 1024], P('seq')
- norm_gain_grad: float32 [1024], replicated
- gate_weight_grad: float32 [1024, 2048], P('seq', 'mp')
- value_weight_grad: float32 [1024, 2048], P('seq', 'mp')
- state_weight_grad: float32 [1024, 288], P('seq')
- conv_value_grad: float32 [5, 2048], replicated
- conv_state_grad: float32 [5, 256], replicated
- head_params_grad: float32 [3, 32], replicated
- gated_gain_grad: float32 [2048], replicated
- out_weight_grad: float32 [1024, 2048], P('seq', 'mp')
- new_norm_gain: float32 [1024], replicated
- new_gate_weight: float32 [1024, 2048], P('seq', 'mp')
- new_value_weight: float32 [1024, 2048], P('seq', 'mp')
- new_state_weight: float32 [1024, 288], P('seq')
- new_conv_value: float32 [5, 2048], replicated
- new_conv_state: float32 [5, 256], replicated
- new_head_params: float32 [3, 32], replicated
- new_gated_gain: float32 [2048], replicated
- new_out_weight: float32 [1024, 2048], P('seq', 'mp')
- new_norm_gain_velocity: float32 [1024], replicated
- new_gate_weight_velocity: float32 [1024, 2048], P('seq', 'mp')
- new_value_weight_velocity: float32 [1024, 2048], P('seq', 'mp')
- new_state_weight_velocity: float32 [1024, 288], P('seq')
- new_conv_value_velocity: float32 [5, 2048], replicated
- new_conv_state_velocity: float32 [5, 256], replicated
- new_head_params_velocity: float32 [3, 32], replicated
- new_gated_gain_velocity: float32 [2048], replicated
- new_out_weight_velocity: float32 [1024, 2048], P('seq', 'mp')
Inputs may be any that keep to these rules, and one draw needn't show every extreme that they name: `head_params`: row 0 holds step biases, row 1 logarithms of decay rates, row 2 skip coefficients.
All inputs are finite; a program needn't handle non-finite values. No bound on the sum of `doc_starts` on one device may be relied on, other than what follows from the above.
Results may differ from a plain program's by a relative error of at most 0.0003.
Values sent between devices are 32-bit elements; how exact they have to be, the bound alone decides.
No kernel may reach another device: no remote copies, remote signals or barrier semaphores. Data moves between devices by JAX's collectives and lax.ppermute only.
A program may use at most 256 MiB of HBM per device.

v0:
```python
import jax
import jax.numpy as jnp
from jax import lax
from jax.sharding import PartitionSpec as P

D = 1024
DI = 2048
H = 32
P_SIZE = 64
N = 128
K = 4
GROUP = 256


highest = lax.Precision.HIGHEST
epsilon = 1e-05
momentum_decay = 0.95
matrix_rate = 0.03
vector_rate = 0.2
quintic_a = 3.4445
quintic_b = -4.775
quintic_c = 2.0315


def passed_along(shard, axis, by):
    size = lax.axis_size(axis)
    pairs = [(i, i + by) for i in range(size) if 0 <= i + by < size]
    return lax.ppermute(shard, axis, pairs)


def carried_in(part, axis, combine, identity, reverse):
    count = lax.axis_size(axis)
    place = lax.axis_index(axis)
    ahead = count - 1 - place if reverse else place
    gathered = jax.tree.map(lambda a: lax.all_gather(a, axis), part)
    state = jax.tree.map(lambda a, e: jnp.zeros_like(a) + jnp.asarray(e, a.dtype), part, identity)

    def one(lap, state):
        source = count - 1 - lap if reverse else lap
        return combine(
            state, jax.tree.map(lambda a: lax.dynamic_index_in_dim(a, source, 0, False), gathered)
        )

    return lax.fori_loop(0, ahead, one, state)


def matmul(left, right):
    return jnp.dot(left, right, precision=highest)


def dot_last(left, right):
    return lax.dot_general(left, right, (((1,), (1,)), ((), ())), precision=highest)


def dot_first(left, right):
    return lax.dot_general(left, right, (((0,), (0,)), ((), ())), precision=highest)


def silu_slope(value):
    sigma = jax.nn.sigmoid(value)
    return sigma * (1.0 + value * (1.0 - sigma))


def chain_combine(earlier, later):
    return (earlier[0] * later[0], later[0][:, None, None] * earlier[1] + later[1])


def gram_of(units):
    return tuple((jnp.einsum("rup,ruq->upq", unit, unit, precision=highest) for unit in units))


def poly_step(units, grams):
    result = []
    for unit, gram in zip(units, grams):
        square = jnp.einsum("upq,uqs->ups", gram, gram, precision=highest)
        result.append(
            quintic_a * unit
            + jnp.einsum(
                "rup,upq->ruq", unit, quintic_b * gram + quintic_c * square, precision=highest
            )
        )
    return tuple(result)


def vector_step(current, gradient, velocity):
    new_velocity = momentum_decay * velocity + gradient
    direction = gradient + momentum_decay * new_velocity
    magnitude = jnp.sqrt(jnp.mean(current * current))
    return (
        current
        - vector_rate * magnitude * direction / jnp.sqrt(jnp.mean(direction * direction) + 1e-06),
        new_velocity,
    )


def body(
    layer_input,
    cotangent,
    doc_starts,
    norm_gain,
    gate_weight,
    value_weight,
    state_weight,
    conv_value,
    conv_state,
    head_params,
    gated_gain,
    out_weight,
    norm_gain_velocity,
    gate_weight_velocity,
    value_weight_velocity,
    state_weight_velocity,
    conv_value_velocity,
    conv_state_velocity,
    head_params_velocity,
    gated_gain_velocity,
    out_weight_velocity,
):
    model_count = lax.axis_size("mp")
    model_index = lax.axis_index("mp")
    rows = layer_input.shape[0]
    local_inner = DI // model_count
    local_heads = H // model_count
    inner_start = model_index * local_inner
    head_start = model_index * local_heads
    block_count = rows // GROUP
    rim = K - 1
    gate_full, value_full, state_full, out_full = (
        lax.all_gather(gate_weight, "seq", axis=0, tiled=True),
        lax.all_gather(value_weight, "seq", axis=0, tiled=True),
        lax.all_gather(state_weight, "seq", axis=0, tiled=True),
        lax.all_gather(out_weight, "seq", axis=0, tiled=True),
    )
    gain_local = lax.dynamic_slice_in_dim(gated_gain, inner_start, local_inner, 0)
    conv_local = jnp.concatenate(
        [lax.dynamic_slice_in_dim(conv_value, inner_start, local_inner, 1), conv_state], 1
    )
    head_local = lax.dynamic_slice_in_dim(head_params, head_start, local_heads, 1)
    starts_float = doc_starts.astype(jnp.float32)
    scale = lax.rsqrt(jnp.mean(layer_input * layer_input, 1, keepdims=True) + epsilon)
    normed = layer_input * scale
    features = normed * norm_gain
    gate = matmul(features, gate_full)
    value_raw = matmul(features, value_full)
    state_raw = matmul(features, state_full)
    mixed_in = jnp.concatenate([value_raw, state_raw[:, : 2 * N]], 1)
    prev_rows, prev_starts = passed_along(
        (mixed_in[rows - rim :], starts_float[rows - rim :]), "seq", 1
    )
    padded = jnp.concatenate([prev_rows, mixed_in], 0)
    cumulative = jnp.cumsum(jnp.concatenate([prev_starts, starts_float]))
    keeps = [jnp.ones((rows,), jnp.float32)]
    for lag in range(1, K):
        keeps.append(
            (cumulative[rim:] - cumulative[rim - lag : rim - lag + rows] < 0.5).astype(jnp.float32)
        )
    conv_pre = conv_local[K] + jnp.zeros_like(mixed_in)
    for lag in range(K):
        conv_pre = (
            conv_pre + keeps[lag][:, None] * conv_local[lag] * padded[rim - lag : rim - lag + rows]
        )
    activated = jax.nn.silu(conv_pre)
    head_values = activated[:, :local_inner].reshape(block_count, GROUP, local_heads, P_SIZE)
    input_map = activated[:, local_inner : local_inner + N].reshape(block_count, GROUP, N)
    read_map = activated[:, local_inner + N :].reshape(block_count, GROUP, N)
    step_pre = (
        lax.dynamic_slice_in_dim(state_raw, 2 * N + head_start, local_heads, 1) + head_local[0]
    )
    step_size = jax.nn.softplus(step_pre)
    rate = -jnp.exp(head_local[1])
    skip = head_local[2]
    step_blocks = step_size.reshape(block_count, GROUP, local_heads)
    log_sums = jnp.cumsum(step_blocks * rate, 1)
    start_blocks = starts_float.reshape(block_count, GROUP)
    segment = jnp.cumsum(start_blocks, 1)
    position = jnp.arange(GROUP)
    same = (position[:, None] >= position[None, :])[None] & (
        segment[:, :, None] == segment[:, None, :]
    )
    causal_mask = same[:, None]
    head_logs = jnp.transpose(log_sums, (0, 2, 1))
    log_gap = head_logs[:, :, :, None] - head_logs[:, :, None, :]
    decay_mat = jnp.where(causal_mask, jnp.exp(jnp.where(causal_mask, log_gap, 0.0)), 0.0)
    scores = jnp.einsum("bin,bjn->bij", read_map, input_map, precision=highest)
    weighted = decay_mat * scores[:, None]
    scaled = head_values * step_blocks[..., None]
    intra = jnp.einsum("bhij,bjhp->bihp", weighted, scaled, precision=highest)
    last_log = log_sums[:, -1]
    last_segment = segment[:, -1]
    tail_weight = (
        jnp.exp(last_log[:, None, :] - log_sums) * (segment == last_segment[:, None])[..., None]
    )
    block_state = jnp.einsum(
        "bjh,bjhp,bjn->bhpn", tail_weight, scaled, input_map, precision=highest
    )
    block_decay = jnp.exp(last_log) * (last_segment == 0)[:, None]
    entry_weight = jnp.exp(log_sums) * (segment == 0)[..., None]
    running = jnp.zeros((local_heads, P_SIZE, N), jnp.float32)
    through = jnp.ones((local_heads,), jnp.float32)
    index = 0
    local_entry = [running]
    prefixes = [through]
    running = block_decay[index][:, None, None] * running + block_state[index]
    through = through * block_decay[index]
    incoming = carried_in(
        (through, running),
        "seq",
        chain_combine,
        (jnp.ones_like(through), jnp.zeros_like(running)),
        False,
    )
    entries = jnp.stack(local_entry) + jnp.stack(prefixes)[:, :, None, None] * incoming[1][None]
    state_read = jnp.einsum("bhpn,bin->bihp", entries, read_map, precision=highest)
    ssd_blocks = (
        intra + entry_weight[..., None] * state_read + head_values * skip[None, None, :, None]
    )
    ssd_out = ssd_blocks.reshape(rows, local_inner)
    gate_act = jax.nn.silu(gate)
    product = ssd_out * gate_act
    square_sum = lax.psum(jnp.sum(product * product, 1), "mp")
    gate_scale = lax.rsqrt(square_sum / DI + epsilon)[:, None]
    gated = product * gate_scale * gain_local
    branch_total = lax.psum(dot_last(gated, out_full), "mp")
    layer_output = layer_input + branch_total
    grad_gated = matmul(cotangent, out_full)
    gated_gain_part = jnp.sum(grad_gated * product * gate_scale, 0)
    grad_hat = grad_gated * gain_local
    inner_sum = jnp.sum(cotangent * branch_total, 1, keepdims=True) / gate_scale
    grad_product = gate_scale * (grad_hat - product * gate_scale * gate_scale * (inner_sum / DI))
    grad_ssd = grad_product * gate_act
    grad_gate = grad_product * ssd_out * silu_slope(gate)
    ssd_grad = grad_ssd.reshape(block_count, GROUP, local_heads, P_SIZE)
    skip_grad = jnp.sum(ssd_grad * head_values, (0, 1, 3))
    grad_values = ssd_grad * skip[None, None, :, None]
    weighted_grad = ssd_grad * entry_weight[..., None]
    enter_grad = jnp.einsum("bihp,bin->bhpn", weighted_grad, read_map, precision=highest)
    read_grad = jnp.einsum("bihp,bhpn->bin", weighted_grad, entries, precision=highest)
    logs_grad = jnp.sum(ssd_grad * state_read, 3) * entry_weight
    mix_grad = jnp.einsum("bihp,bjhp->bhij", ssd_grad, scaled, precision=highest)
    scaled_grad = jnp.einsum("bhij,bihp->bjhp", weighted, ssd_grad, precision=highest)
    score_grad = jnp.sum(mix_grad * decay_mat, 1)
    read_grad = read_grad + jnp.einsum("bij,bjn->bin", score_grad, input_map, precision=highest)
    input_grad_map = jnp.einsum("bij,bin->bjn", score_grad, read_map, precision=highest)
    decay_term = mix_grad * weighted
    logs_grad = logs_grad + jnp.transpose(
        jnp.sum(decay_term, 3) - jnp.sum(decay_term, 2), (0, 2, 1)
    )
    local_out = [None] * block_count
    after = [None] * block_count
    carry_grad = jnp.zeros((local_heads, P_SIZE, N), jnp.float32)
    carry_decay = jnp.ones((local_heads,), jnp.float32)
    for index in reversed(range(block_count)):
        local_out[index] = carry_grad
        after[index] = carry_decay
        carry_grad = enter_grad[index] + block_decay[index][:, None, None] * carry_grad
        carry_decay = carry_decay * block_decay[index]
    later = carried_in(
        (carry_decay, carry_grad),
        "seq",
        chain_combine,
        (jnp.ones_like(carry_decay), jnp.zeros_like(carry_grad)),
        True,
    )
    out_grads = jnp.stack(local_out) + jnp.stack(after)[:, :, None, None] * later[1][None]
    scaled_grad = scaled_grad + tail_weight[..., None] * jnp.einsum(
        "bhpn,bjn->bjhp", out_grads, input_map, precision=highest
    )
    input_grad_map = input_grad_map + jnp.einsum(
        "bhpn,bjhp->bjn", out_grads, scaled * tail_weight[..., None], precision=highest
    )
    tail_grad = (
        jnp.einsum("bhpn,bjhp,bjn->bjh", out_grads, scaled, input_map, precision=highest)
        * tail_weight
    )
    last_grad = jnp.sum(tail_grad, 1) + jnp.sum(out_grads * entries, (2, 3)) * block_decay
    logs_grad = (
        logs_grad
        - tail_grad
        + jnp.concatenate(
            [jnp.zeros((block_count, GROUP - 1, local_heads), jnp.float32), last_grad[:, None]], 1
        )
    )
    decay_log_grad = jnp.flip(jnp.cumsum(jnp.flip(logs_grad, 1), 1), 1)
    grad_values = grad_values + scaled_grad * step_blocks[..., None]
    step_grad = jnp.sum(scaled_grad * head_values, 3) + decay_log_grad * rate
    rate_grad = jnp.sum(decay_log_grad * step_blocks, (0, 1))
    log_rate_grad = rate_grad * rate
    step_pre_grad = step_grad.reshape(rows, local_heads) * jax.nn.sigmoid(step_pre)
    bias_grad = jnp.sum(step_pre_grad, 0)
    map_grad = jnp.concatenate([input_grad_map.reshape(rows, N), read_grad.reshape(rows, N)], 1)
    step_full = lax.dynamic_update_slice_in_dim(
        jnp.zeros((rows, H), jnp.float32), step_pre_grad, head_start, 1
    )
    map_grad, step_full = lax.psum((map_grad, step_full), "mp")
    act_grad = jnp.concatenate([grad_values.reshape(rows, local_inner), map_grad], 1)
    pre_grad = act_grad * silu_slope(conv_pre)
    conv_rows = []
    padded_grad = jnp.zeros_like(padded)
    for lag in range(K):
        masked = keeps[lag][:, None] * pre_grad
        conv_rows.append(jnp.sum(masked * padded[rim - lag : rim - lag + rows], 0))
        padded_grad = padded_grad + jnp.pad(masked * conv_local[lag], ((rim - lag, lag), (0, 0)))
    conv_rows.append(jnp.sum(pre_grad, 0))
    conv_local_grad = jnp.stack(conv_rows)
    spill = passed_along(padded_grad[:rim], "seq", -1)
    mixed_grad = padded_grad[rim:] + jnp.pad(spill, ((rows - rim, 0), (0, 0)))
    value_raw_grad = mixed_grad[:, :local_inner]
    state_raw_grad = jnp.concatenate([mixed_grad[:, local_inner:], step_full], 1)
    features_part = (
        dot_last(grad_gate, gate_full)
        + dot_last(value_raw_grad, value_full)
        + dot_last(state_raw_grad, state_full) / model_count
    )
    features_grad = lax.psum(features_part, "mp")
    norm_gain_part = jnp.sum(features_part * normed, 0)
    gain_grad_in = features_grad * norm_gain
    input_grad = cotangent + scale * (
        gain_grad_in - normed * jnp.mean(gain_grad_in * normed, 1, keepdims=True)
    )
    right_columns = jnp.concatenate([grad_gate, value_raw_grad, state_raw_grad], 1)
    reduced = lax.psum_scatter(
        jnp.concatenate([dot_first(features, right_columns), dot_first(cotangent, gated)], 1),
        "seq",
        scatter_dimension=0,
        tiled=True,
    )
    gate_weight_grad = reduced[:, :local_inner]
    value_weight_grad = reduced[:, local_inner : 2 * local_inner]
    state_weight_grad = reduced[:, 2 * local_inner : 2 * local_inner + 2 * N + H]
    out_weight_grad = reduced[:, 2 * local_inner + 2 * N + H :]
    conv_value_part = lax.dynamic_update_slice_in_dim(
        jnp.zeros((K + 1, DI), jnp.float32), conv_local_grad[:, :local_inner], inner_start, 1
    )
    conv_state_part = conv_local_grad[:, local_inner:] / model_count
    head_part = lax.dynamic_update_slice_in_dim(
        jnp.zeros((3, H), jnp.float32),
        jnp.stack([bias_grad, log_rate_grad, skip_grad]),
        head_start,
        1,
    )
    gated_part = lax.dynamic_update_slice_in_dim(
        jnp.zeros((DI,), jnp.float32), gated_gain_part, inner_start, 0
    )
    norm_gain_grad, conv_value_grad, conv_state_grad, head_params_grad, gated_gain_grad = lax.psum(
        (norm_gain_part, conv_value_part, conv_state_part, head_part, gated_part), ("seq", "mp")
    )
    matrix_grads = (gate_weight_grad, value_weight_grad, state_weight_grad, out_weight_grad)
    matrix_velocities = (
        gate_weight_velocity,
        value_weight_velocity,
        state_weight_velocity,
        out_weight_velocity,
    )
    new_velocities = tuple(
        (
            momentum_decay * velocity + gradient
            for gradient, velocity in zip(matrix_grads, matrix_velocities)
        )
    )
    updates = tuple(
        (
            gradient + momentum_decay * velocity
            for gradient, velocity in zip(matrix_grads, new_velocities)
        )
    )
    owned = updates[0].shape[0]
    head_units = jnp.concatenate(
        [
            updates[0].reshape(owned, local_heads, P_SIZE),
            updates[1].reshape(owned, local_heads, P_SIZE),
            updates[3].reshape(owned, local_heads, P_SIZE),
        ],
        1,
    )
    map_units = updates[2][:, : 2 * N].reshape(owned, 2, N)
    step_units = updates[2][:, 2 * N :].reshape(owned, 1, H)
    units = (head_units, map_units, step_units)
    current = units
    for sweep in range(5):
        grams = lax.psum(gram_of(current), "seq")
        if sweep == 0:
            norms = tuple((jnp.sqrt(jnp.trace(gram, axis1=1, axis2=2)) + 1e-07 for gram in grams))
            current = tuple((unit / norm[None, :, None] for unit, norm in zip(current, norms)))
            grams = tuple((gram / (norm * norm)[:, None, None] for gram, norm in zip(grams, norms)))
        current = poly_step(current, grams)
    factor = matrix_rate * 0.2 * D**0.5
    head_orth = current[0]
    gate_orth = head_orth[:, :local_heads].reshape(owned, local_inner)
    value_orth = head_orth[:, local_heads : 2 * local_heads].reshape(owned, local_inner)
    out_orth = head_orth[:, 2 * local_heads :].reshape(owned, local_inner)
    state_orth = jnp.concatenate(
        [current[1].reshape(owned, 2 * N), current[2].reshape(owned, H)], 1
    )
    new_gate_weight = gate_weight - factor * gate_orth
    new_value_weight = value_weight - factor * value_orth
    new_state_weight = state_weight - factor * state_orth
    new_out_weight = out_weight - factor * out_orth
    new_norm_gain, new_norm_velocity = vector_step(norm_gain, norm_gain_grad, norm_gain_velocity)
    new_conv_value, new_conv_value_velocity = vector_step(
        conv_value, conv_value_grad, conv_value_velocity
    )
    new_conv_state, new_conv_state_velocity = vector_step(
        conv_state, conv_state_grad, conv_state_velocity
    )
    new_head_params, new_head_velocity = vector_step(
        head_params, head_params_grad, head_params_velocity
    )
    new_gated_gain, new_gated_velocity = vector_step(
        gated_gain, gated_gain_grad, gated_gain_velocity
    )
    return (
        layer_output,
        input_grad,
        norm_gain_grad,
        gate_weight_grad,
        value_weight_grad,
        state_weight_grad,
        conv_value_grad,
        conv_state_grad,
        head_params_grad,
        gated_gain_grad,
        out_weight_grad,
        new_norm_gain,
        new_gate_weight,
        new_value_weight,
        new_state_weight,
        new_conv_value,
        new_conv_state,
        new_head_params,
        new_gated_gain,
        new_out_weight,
        new_norm_velocity,
        new_velocities[0],
        new_velocities[1],
        new_velocities[2],
        new_conv_value_velocity,
        new_conv_state_velocity,
        new_head_velocity,
        new_gated_velocity,
        new_velocities[3],
    )


def solution(mesh):
    return jax.shard_map(
        body,
        mesh=mesh,
        in_specs=(
            P("seq", None),
            P("seq", None),
            P("seq"),
            P(),
            P("seq", "mp"),
            P("seq", "mp"),
            P("seq", None),
            P(),
            P(),
            P(),
            P(),
            P("seq", "mp"),
            P(),
            P("seq", "mp"),
            P("seq", "mp"),
            P("seq", None),
            P(),
            P(),
            P(),
            P(),
            P("seq", "mp"),
        ),
        out_specs=(
            P("seq", None),
            P("seq", None),
            P(),
            P("seq", "mp"),
            P("seq", "mp"),
            P("seq", None),
            P(),
            P(),
            P(),
            P(),
            P("seq", "mp"),
            P(),
            P("seq", "mp"),
            P("seq", "mp"),
            P("seq", None),
            P(),
            P(),
            P(),
            P(),
            P("seq", "mp"),
            P(),
            P("seq", "mp"),
            P("seq", "mp"),
            P("seq", None),
            P(),
            P(),
            P(),
            P(),
            P("seq", "mp"),
        ),
        check_vma=False,
    )
```

profile of v0, /device:TPU:0, one launch (start us, length us, event | category | flops | bytes accessed | tf_op | source)
XLA Modules:
  0.0 1663.4 jit_solution(13704015981688323734)
XLA Ops:
  23.5 48.0 %all-gather.12.cloned.1.call-done = f32[1024,288]{1,0:T(8,128)} async-done(((f32[64,288]{1,0:T(8,128)}), f32[1024,288]{1,0:T(8,128)}) %all-gather.12.cloned.1.call-update) | async-done | bytes 1179664 | tf_op jit(solution)/shard_map/all_gather | solution.py:131
  78.3 70.4 %all-gather.10.cloned.1.call-done = f32[1024,1024]{1,0:T(8,128)} async-done(((f32[64,1024]{1,0:T(8,128)}), f32[1024,1024]{1,0:T(8,128)}) %all-gather.10.cloned.1.call-update) | async-done | bytes 4194320 | tf_op jit(solution)/shard_map/all_gather | solution.py:130
  175.7 41.1 %all-gather = f32[16,1,16]{2,1,0:T(1,128)} all-gather(f32[1,1,16]{2,1,0:T(1,128)} %get-tuple-element.508), channel_id=2, replica_groups=mesh['seq'=16,'mp'=2] {'seq'}, dimensions={0}, use_global_device_ids=true | all-gather | bytes 1088 | tf_op jit(solution)/shard_map/all_gather | solution.py:35
  219.0 63.9 %all-gather.18.cloned.1.call-done = f32[256,64,128]{2,1,0:T(8,128)} async-done(((f32[16,64,128]{2,1,0:T(8,128)}), f32[256,64,128]{2,1,0:T(8,128)}) %all-gather.18.cloned.1.call-update) | async-done | bytes 8388624 | tf_op jit(solution)/shard_map/all_gather | solution.py:35
  294.1 65.3 %all-gather.14.cloned.1.call-done = f32[1024,1024]{1,0:T(8,128)} async-done(((f32[64,1024]{1,0:T(8,128)}), f32[1024,1024]{1,0:T(8,128)}) %all-gather.14.cloned.1.call-update) | async-done | bytes 4194320 | tf_op jit(solution)/shard_map/all_gather | solution.py:129
  359.3 7.6 multiply_reduce_fusion.13
  369.4 66.8 %all-gather.16.cloned.1.call-done = f32[1024,1024]{1,0:T(8,128)} async-done(((f32[64,1024]{1,0:T(8,128)}), f32[1024,1024]{1,0:T(8,128)}) %all-gather.16.cloned.1.call-update) | async-done | bytes 4194320 | tf_op jit(solution)/shard_map/all_gather | solution.py:132
  463.8 10.5 multiply_reduce_fusion.7
  496.9 8.1 fusion.6
  519.4 76.2 %all-gather.20.cloned.1.call-done = f32[256,64,128]{2,1,0:T(8,128)} async-done(((f32[16,64,128]{2,1,0:T(8,128)}), f32[256,64,128]{2,1,0:T(8,128)}) %all-gather.20.cloned.1.call-update) | async-done | bytes 8388624 | tf_op jit(solution)/shard_map/all_gather | solution.py:35
  595.7 28.5 %while.27 = (s32[]{:T(128)}, f32[16,64,128]{2,1,0:T(8,128)S(1)}, s32[]{:T(128)}, f32[16,16]{1,0:T(8,128)}, f32[16,16,64,128]{3,2,1,0:T(8,128)}, /*index=5*/s32[]{:T(128)}, s32[]{:T(128)}, s32[]{:T(128)}, s32[]{:T(128)}) while((s32[]{:T(128)}, f32[16,64,128]{2,1,0:T(8,128)S(1)}, s32[]{:T(128)}, f32[16,16]{1,0:T(8,128)}, ...), condition=%wide.region_14.15_spmd, body=%wide.region_13.14_spmd.sunk | while | flops 262150 | bytes 1573211 | solution.py:44
  678.9 9.1 fusion.8
  688.0 8.3 pad_maximum_fusion
  696.3 14.8 copy.610
  722.1 40.9 %all-reduce.7 = (f32[1024]{0:T(1024)S(1)}, f32[5,2048]{1,0:T(8,128)}, f32[5,256]{1,0:T(8,128)S(1)}, f32[3,32]{1,0:T(4,128)S(1)}, f32[2048]{0:T(1024)S(1)}) all-reduce(f32[1024]{0:T(1024)S(1)} %get-tuple-element.409, f32[5,2048]{1,0:T(8,128)S(1)} %slice_dynamic-update-slice_fusion, ...), channel_id=1, replica_groups=mesh['seq'=16,'mp'=2] {'seq','mp'}, use_global_device_ids=true, to_apply=%region_29.30 | all-reduce | flops 14688 | bytes 117504 | tf_op jit(solution)/shard_map/psum | solution.py:344
  763.0 166.0 %reduce-scatter.4.cloned.1.call-done = f32[64,3360]{1,0:T(8,128)} async-done(((f32[1024,3360]{1,0:T(8,128)}), f32[64,3360]{1,0:T(8,128)}) %reduce-scatter.4.cloned.1.call-update) | async-done | bytes 860176 | tf_op jit(solution)/shard_map/reduce_scatter | solution.py:321
  949.8 113.7 %all-reduce.36.cloned.1.call-done = (f32[48,64,64]{2,1,0:T(8,128)}, f32[2,128,128]{2,1,0:T(8,128)}) async-done(((f32[48,64,64]{2,1,0:T(8,128)}, f32[2,128,128]{2,1,0:T(8,128)}), (f32[48,64,64]{2,1,0:T(8,128)}, f32[2,128,128]{2,1,0:T(8,128)})) %all-reduce.36.cloned.1.call-update) | async-done | bytes 917520 | tf_op jit(solution)/shard_map/psum | solution.py:380
  1082.4 112.1 %all-reduce.34.cloned.1.call-done = (f32[48,64,64]{2,1,0:T(8,128)}, f32[2,128,128]{2,1,0:T(8,128)}) async-done(((f32[48,64,64]{2,1,0:T(8,128)}, f32[2,128,128]{2,1,0:T(8,128)}), (f32[48,64,64]{2,1,0:T(8,128)}, f32[2,128,128]{2,1,0:T(8,128)})) %all-reduce.34.cloned.1.call-update) | async-done | bytes 917520 | tf_op jit(solution)/shard_map/psum | solution.py:380
  1209.9 75.5 %psum.195 = f32[1,32,32]{2,1,0:T(8,128)S(1)} all-reduce(f32[1,32,32]{2,1,0:T(8,128)S(1)} %convolution_bitcast_fusion.17), channel_id=1, replica_groups=mesh['seq'=16,'mp'=2] {'seq'}, use_global_device_ids=true, to_apply=%region_59.60 | all-reduce | flops 1024 | bytes 8192 | tf_op jit(solution)/shard_map/psum | solution.py:380
  1286.7 38.7 %all-reduce.32.cloned.1.call-done = (f32[48,64,64]{2,1,0:T(8,128)}, f32[2,128,128]{2,1,0:T(8,128)}) async-done(((f32[48,64,64]{2,1,0:T(8,128)}, f32[2,128,128]{2,1,0:T(8,128)}), (f32[48,64,64]{2,1,0:T(8,128)}, f32[2,128,128]{2,1,0:T(8,128)})) %all-reduce.32.cloned.1.call-update) | async-done | bytes 917520 | tf_op jit(solution)/shard_map/psum | solution.py:380
  1337.8 75.6 %psum.196 = f32[1,32,32]{2,1,0:T(8,128)S(1)} all-reduce(f32[1,32,32]{2,1,0:T(8,128)S(1)} %convolution_bitcast_fusion.15), channel_id=1, replica_groups=mesh['seq'=16,'mp'=2] {'seq'}, use_global_device_ids=true, to_apply=%region_61.62 | all-reduce | flops 1024 | bytes 8192 | tf_op jit(solution)/shard_map/psum | solution.py:380
  1413.9 72.6 %psum.197 = f32[1,32,32]{2,1,0:T(8,128)S(1)} all-reduce(f32[1,32,32]{2,1,0:T(8,128)S(1)} %convolution_bitcast_fusion.13), channel_id=1, replica_groups=mesh['seq'=16,'mp'=2] {'seq'}, use_global_device_ids=true, to_apply=%region_62.63 | all-reduce | flops 1024 | bytes 8192 | tf_op jit(solution)/shard_map/psum | solution.py:380
  1498.1 72.6 %psum.198 = f32[1,32,32]{2,1,0:T(8,128)S(1)} all-reduce(f32[1,32,32]{2,1,0:T(8,128)S(1)} %convolution_bitcast_fusion.11), channel_id=1, replica_groups=mesh['seq'=16,'mp'=2] {'seq'}, use_global_device_ids=true, to_apply=%region_63.64 | all-reduce | flops 1024 | bytes 8192 | tf_op jit(solution)/shard_map/psum | solution.py:380
  1571.3 72.9 %psum.199 = f32[1,32,32]{2,1,0:T(8,128)S(1)} all-reduce(f32[1,32,32]{2,1,0:T(8,128)S(1)} %convolution_bitcast_fusion.9), channel_id=1, replica_groups=mesh['seq'=16,'mp'=2] {'seq'}, use_global_device_ids=true, to_apply=%region_64.65 | all-reduce | flops 1024 | bytes 8192 | tf_op jit(solution)/shard_map/psum | solution.py:380
  (523 shorter events, 307.5 us)
Async XLA Ops:
  7.2 64.3 %all-gather.12.cloned.1.call-start = ((), (), s32[]{:S(2)}) async-start(), calls=%async_computation.2 | async-start | bytes 1671168 | tf_op jit(solution)/shard_map/all_gather | solution.py:131
  8.0 140.7 %all-gather.10.cloned.1.call-start = ((), (), s32[]{:S(2)}) async-start(), calls=%async_computation.1 | async-start | bytes 4456448 | tf_op jit(solution)/shard_map/all_gather | solution.py:130
  8.7 274.2 %all-gather.18.cloned.1.call-start = ((), (), s32[]{:S(2)}) async-start(), calls=%async_computation.8 | async-start | bytes 8912896 | tf_op jit(solution)/shard_map/all_gather | solution.py:35
  9.5 12.6 collective-permute-start
  154.5 4.8 collective-permute-start.1
  169.9 189.4 %all-gather.14.cloned.1.call-start = ((), (), s32[]{:S(2)}) async-start(), calls=%async_computation.3 | async-start | bytes 4456448 | tf_op jit(solution)/shard_map/all_gather | solution.py:129
  170.5 265.6 %all-gather.16.cloned.1.call-start = ((), (), s32[]{:S(2)}) async-start(), calls=%async_computation.4 | async-start | bytes 4456448 | tf_op jit(solution)/shard_map/all_gather | solution.py:132
  171.1 290.5 %all-reduce.22.cloned.1.call-start = ((), (), s32[]{:S(2)}) async-start(), calls=%async_computation.5 | async-start | bytes 2097152 | tf_op jit(solution)/shard_map/psum | solution.py:223
  219.0 277.9 %copy-start.52 = (f32[256,256]{1,0:T(8,128)}, f32[256,256]{1,0:T(8,128)S(1)}, u32[]{:S(2)}) copy-start(f32[256,256]{1,0:T(8,128)S(1)} %fusion.175) | copy-start | bytes 786436
  443.4 152.2 %all-gather.20.cloned.1.call-start = ((), (), s32[]{:S(2)}) async-start(), calls=%async_computation.9 | async-start | bytes 8912896 | tf_op jit(solution)/shard_map/all_gather | solution.py:35
  482.0 180.0 %all-reduce.24.cloned.1.call-start = ((), (), s32[]{:S(2)}) async-start(), calls=%async_computation.6 | async-start | bytes 524288 | tf_op jit(solution)/shard_map/psum | solution.py:294
  632.6 87.3 %all-reduce.26.cloned.1.call-start = ((), (), s32[]{:S(2)}) async-start(), calls=%async_computation.7 | async-start | bytes 2097152 | tf_op jit(solution)/shard_map/psum | solution.py:314
  666.0 5.7 collective-permute-start.2
  678.6 250.3 %reduce-scatter.4.cloned.1.call-start = ((), (), s32[]{:S(2)}) async-start(), calls=%async_computation.10 | async-start | bytes 15040512 | tf_op jit(solution)/shard_map/reduce_scatter | solution.py:321
  711.2 352.3 %all-reduce.36.cloned.1.call-start = ((), (), s32[]{:S(2)}) async-start(), calls=%async_computation.15 | async-start | bytes 3407872 | tf_op jit(solution)/shard_map/psum | solution.py:380
  719.8 209.1 %copy-start.56 = (f32[64,1024]{1,0:T(8,128)S(1)}, f32[64,1024]{1,0:T(8,128)}, u32[]{:S(2)}) copy-start(f32[64,1024]{1,0:T(8,128)} %param.45) | copy-start | bytes 786436
  719.8 209.1 %copy-start.57 = (f32[64,1024]{1,0:T(8,128)S(1)}, f32[64,1024]{1,0:T(8,128)}, u32[]{:S(2)}) copy-start(f32[64,1024]{1,0:T(8,128)} %param.39) | copy-start | bytes 786436
  763.0 183.7 %copy-start.78 = (f32[1024]{0:T(1024)}, f32[1024]{0:T(1024)S(1)}, u32[]{:S(2)}) copy-start(f32[1024]{0:T(1024)S(1)} %get-tuple-element.436) | copy-start | bytes 12292
  763.0 314.3 %copy-start.68 = (f32[5,256]{1,0:T(8,128)}, f32[5,256]{1,0:T(8,128)S(1)}, u32[]{:S(2)}) copy-start(f32[5,256]{1,0:T(8,128)S(1)} %get-tuple-element.438) | copy-start | bytes 15364
  763.0 444.7 %copy-start.69 = (f32[2048]{0:T(1024)}, f32[2048]{0:T(1024)S(1)}, u32[]{:S(2)}) copy-start(f32[2048]{0:T(1024)S(1)} %get-tuple-element.440) | copy-start | bytes 24580
  943.9 250.6 %all-reduce.34.cloned.1.call-start = ((), (), s32[]{:S(2)}) async-start(), calls=%async_computation.14 | async-start | bytes 3407872 | tf_op jit(solution)/shard_map/psum | solution.py:380
  1075.4 250.0 %all-reduce.32.cloned.1.call-start = ((), (), s32[]{:S(2)}) async-start(), calls=%async_computation.13 | async-start | bytes 3407872 | tf_op jit(solution)/shard_map/psum | solution.py:380
  1205.6 281.1 %all-reduce.30.cloned.1.call-start = ((), (), s32[]{:S(2)}) async-start(), calls=%async_computation.12 | async-start | bytes 3407872 | tf_op jit(solution)/shard_map/psum | solution.py:380
  1336.4 308.9 %all-reduce.28.cloned.1.call-start = ((), (), s32[]{:S(2)}) async-start(), calls=%async_computation.11 | async-start | bytes 3407872 | tf_op jit(solution)/shard_map/psum | solution.py:380
  (102 other events, 2070.4 us)
Sparse Core Ops, SparseCore 0:
  10.8 60.6 all-gather.11
  74.3 74.3 all-gather.9
  170.1 112.7 all-gather.17
  285.5 73.7 all-gather.13
  361.9 74.1 all-gather.15
  443.5 18.0 all-reduce.21
  482.1 113.4 all-gather.19
  632.7 14.0 all-reduce.23
  678.8 15.8 all-reduce.25
  711.3 217.6 reduce-scatter.3
  944.0 119.4 all-reduce.35
  1075.5 118.9 all-reduce.33
  1205.7 119.6 all-reduce.31
  1336.6 119.8 all-reduce.29
  1497.9 116.5 all-reduce.27
where the time goes:
time: 1670 us; the launch traced here: 1660 us
  waiting for transfers between devices  835 us (50%)
  blocking collectives  459 us (27%)
  matrix products  167 us (10%)
  local copies, waits for them, and re-layouts  82.2 us (5%)
  other arithmetic  81.9 us (5%)
  between operations  24.8 us (1%)
    psum x5, blocking collectives, body(): grams = lax.psum(gram_of(current), 'seq')  369 us
    psum x5, waiting for transfers between devices, body(): grams = lax.psum(gram_of(current), 'seq')  264 us
    reduce_scatter x1, waiting for transfers between devices, body(): lax.psum_scatter(jnp.concatenate([dot_first(features, right_columns), dot...  166 us
    all_gather x2, waiting for transfers between devices, carried_in(): gathered = jax.tree.map(lambda a: lax.all_gather(a, axis), part)  140 us
    all_gather x1, waiting for transfers between devices, body(): lax.all_gather(value_weight, 'seq', axis=0, tiled=True)  70.4 us
    all_gather x1, waiting for transfers between devices, body(): lax.all_gather(out_weight, 'seq', axis=0, tiled=True)  66.8 us
    all_gather x1, waiting for transfers between devices, body(): lax.all_gather(gate_weight, 'seq', axis=0, tiled=True)  65.3 us
    all_gather x1, waiting for transfers between devices, body(): lax.all_gather(state_weight, 'seq', axis=0, tiled=True)  48 us
  transfers between devices with their start and end apart: 18, of which 13 were waited for; matrix products, arithmetic and copies ran while one was open for 10% of the time, Pallas kernels for 0%

commit v1 on v0

v1 whole, which is shorter than its diff:
```python
import functools

import jax
import jax.numpy as jnp
from jax import lax
from jax.experimental import pallas as pl
from jax.experimental.pallas import tpu as pltpu
from jax.sharding import PartitionSpec as P

D = 1024
DI = 2048
H = 32
P_SIZE = 64
N = 128
K = 4
LANES = 128


highest = lax.Precision.HIGHEST
high = lax.Precision.HIGH
epsilon = 1e-05
momentum_decay = 0.95
matrix_rate = 0.03
vector_rate = 0.2
quintic_a = 3.4445
quintic_b = -4.775
quintic_c = 2.0315


def passed_along(shard, axis, by):
    size = lax.axis_size(axis)
    pairs = [(i, i + by) for i in range(size) if 0 <= i + by < size]
    return lax.ppermute(shard, axis, pairs)


def swapped(shard):
    return lax.ppermute(shard, "mp", [(0, 1), (1, 0)])


def pair_sum(shard):
    return shard + swapped(shard)


def exchange(array):
    return lax.all_to_all(array, "seq", 0, 0, tiled=True)


def matmul(left, right):
    return jnp.dot(left, right, precision=high)


def dot_last(left, right):
    return lax.dot_general(left, right, (((1,), (1,)), ((), ())), precision=high)


def dot_first(left, right):
    return lax.dot_general(left, right, (((0,), (0,)), ((), ())), precision=high)


def silu_slope(value):
    sigma = jax.nn.sigmoid(value)
    return sigma * (1.0 + value * (1.0 - sigma))


def carry_kernel(reverse, part_ref, out_ref):
    count, rows, _ = out_ref.shape

    def one(lap, state):
        source = count - 1 - lap if reverse else lap
        out_ref[source] = state
        return part_ref[source, rows : rows + 1] * state + part_ref[source, :rows]

    lax.fori_loop(0, count, one, jnp.zeros((rows, N), jnp.float32))


def carried_in(decay, state, reverse):
    count = lax.axis_size("seq")
    heads = state.shape[0]
    rows = heads * P_SIZE // count
    owner = jnp.repeat(decay, P_SIZE).reshape(count, rows)[:, :1]
    part = jnp.concatenate(
        [state.reshape(count, rows, N), jnp.broadcast_to(owner[:, :, None], (count, 8, N))], 1
    )
    gathered = exchange(part)
    entering = pl.pallas_call(
        functools.partial(carry_kernel, reverse),
        out_shape=jax.ShapeDtypeStruct((count, rows, N), jnp.float32),
        name="carry",
    )(gathered)
    return exchange(entering).reshape(heads, P_SIZE, N)


def chain_kernel(gram_ref, out_ref):
    count, size, _ = gram_ref.shape
    row = lax.broadcasted_iota(jnp.int32, (size, size), 0)
    col = lax.broadcasted_iota(jnp.int32, (size, size), 1)
    eye = (row == col).astype(jnp.float32)
    grams = []
    totals = []
    for unit in range(count):
        gram = gram_ref[unit]
        norm = jnp.sqrt(jnp.sum(gram * eye, keepdims=True)) + 1e-07
        grams.append(gram / (norm * norm))
        totals.append(eye / norm)
    for sweep in range(5):
        squares = [jnp.dot(gram, gram, precision=highest) for gram in grams]
        steps = [
            quintic_a * eye + quintic_b * gram + quintic_c * square
            for gram, square in zip(grams, squares)
        ]
        totals = [
            jnp.dot(total, step, precision=highest) for total, step in zip(totals, steps)
        ]
        if sweep < 4:
            halves = [
                jnp.dot(step, gram, precision=highest) for step, gram in zip(steps, grams)
            ]
            grams = [
                jnp.dot(half, step, precision=highest) for half, step in zip(halves, steps)
            ]
    for unit in range(count):
        out_ref[unit] = totals[unit]


def chain(grams):
    return pl.pallas_call(
        chain_kernel,
        out_shape=jax.ShapeDtypeStruct(grams.shape, jnp.float32),
        name="chain",
    )(grams)


def padded_to(array, multiple):
    extra = -array.shape[0] % multiple
    return jnp.pad(array, ((0, extra),) + ((0, 0),) * (array.ndim - 1))


def head_grams(update):
    split = update.reshape(update.shape[0], -1, P_SIZE)
    return jnp.einsum("rup,ruq->upq", split, split, precision=highest)


def apply_heads(update, polynomials):
    split = update.reshape(update.shape[0], -1, P_SIZE)
    return jnp.einsum("rup,upq->ruq", split, polynomials, precision=highest).reshape(update.shape)


def vector_step(current, gradient, velocity):
    new_velocity = momentum_decay * velocity + gradient
    direction = gradient + momentum_decay * new_velocity
    magnitude = jnp.sqrt(jnp.mean(current * current))
    return (
        current
        - vector_rate * magnitude * direction / jnp.sqrt(jnp.mean(direction * direction) + 1e-06),
        new_velocity,
    )


def matrix_momentum(gradient, velocity):
    new_velocity = momentum_decay * velocity + gradient
    return new_velocity, gradient + momentum_decay * new_velocity


def body(
    layer_input,
    cotangent,
    doc_starts,
    norm_gain,
    gate_weight,
    value_weight,
    state_weight,
    conv_value,
    conv_state,
    head_params,
    gated_gain,
    out_weight,
    norm_gain_velocity,
    gate_weight_velocity,
    value_weight_velocity,
    state_weight_velocity,
    conv_value_velocity,
    conv_state_velocity,
    head_params_velocity,
    gated_gain_velocity,
    out_weight_velocity,
):
    seq_count = lax.axis_size("seq")
    model_count = lax.axis_size("mp")
    model_index = lax.axis_index("mp")
    rows = layer_input.shape[0]
    inner = DI // model_count
    heads = H // model_count
    inner_start = model_index * inner
    head_start = model_index * heads
    rim = K - 1
    mixed_full = lax.all_gather(
        jnp.concatenate([value_weight, state_weight], 1), "seq", axis=0, tiled=True
    )
    outer_full = lax.all_gather(
        jnp.concatenate([gate_weight, out_weight], 1), "seq", axis=0, tiled=True
    )
    gain_local = lax.dynamic_slice_in_dim(gated_gain, inner_start, inner, 0)
    conv_local = jnp.concatenate(
        [lax.dynamic_slice_in_dim(conv_value, inner_start, inner, 1), conv_state], 1
    )
    head_local = lax.dynamic_slice_in_dim(head_params, head_start, heads, 1)
    starts_float = doc_starts.astype(jnp.float32)
    scale = lax.rsqrt(jnp.mean(layer_input * layer_input, 1, keepdims=True) + epsilon)
    normed = layer_input * scale
    features = normed * norm_gain
    raw = matmul(features, mixed_full)
    mixed_in = raw[:, : inner + 2 * N]
    prev_starts = passed_along(starts_float[rows - rim :], "seq", 1)
    prev_rows = passed_along(mixed_in[rows - rim :], "seq", 1)
    padded = jnp.concatenate([prev_rows, mixed_in], 0)
    cumulative = jnp.cumsum(jnp.concatenate([prev_starts, starts_float]))
    keeps = [jnp.ones((rows,), jnp.float32)]
    for lag in range(1, K):
        keeps.append(
            (cumulative[rim:] - cumulative[rim - lag : rim - lag + rows] < 0.5).astype(jnp.float32)
        )
    conv_pre = conv_local[K] + jnp.zeros_like(mixed_in)
    for lag in range(K):
        conv_pre = (
            conv_pre + keeps[lag][:, None] * conv_local[lag] * padded[rim - lag : rim - lag + rows]
        )
    activated = jax.nn.silu(conv_pre)
    head_values = activated[:, :inner].reshape(rows, heads, P_SIZE)
    input_map = activated[:, inner : inner + N]
    read_map = activated[:, inner + N :]
    step_pre = (
        lax.dynamic_slice_in_dim(raw, inner + 2 * N + head_start, heads, 1) + head_local[0]
    )
    step_size = jax.nn.softplus(step_pre)
    rate = -jnp.exp(head_local[1])
    skip = head_local[2]
    log_sums = jnp.cumsum(step_size * rate, 0)
    segment = jnp.cumsum(starts_float)
    position = jnp.arange(rows)
    causal_mask = (
        (position[:, None] >= position[None, :]) & (segment[:, None] == segment[None, :])
    )[None]
    head_logs = log_sums.T
    log_gap = head_logs[:, :, None] - head_logs[:, None, :]
    decay_mat = jnp.where(causal_mask, jnp.exp(jnp.where(causal_mask, log_gap, 0.0)), 0.0)
    scores = dot_last(read_map, input_map)
    weighted = decay_mat * scores[None]
    scaled = head_values * step_size[..., None]
    last_log = log_sums[-1]
    last_segment = segment[-1]
    tail_weight = jnp.exp(last_log[None] - log_sums) * (segment == last_segment)[:, None]
    tail_scaled = scaled * tail_weight[..., None]
    block_state = jnp.einsum("jhp,jn->hpn", tail_scaled, input_map, precision=high)
    block_decay = jnp.exp(last_log) * (last_segment == 0)
    entry_weight = jnp.exp(log_sums) * (segment == 0)[:, None]
    entries = carried_in(block_decay, block_state, False)
    intra = jnp.einsum("hij,jhp->ihp", weighted, scaled, precision=high)
    state_read = jnp.einsum("hpn,in->ihp", entries, read_map, precision=high)
    ssd_out = (
        intra + entry_weight[..., None] * state_read + head_values * skip[None, :, None]
    ).reshape(rows, inner)
    gate_full = outer_full[:, :inner]
    out_full = outer_full[:, inner:]
    gate = matmul(features, gate_full)
    grad_gated = matmul(cotangent, out_full)
    grad_hat = grad_gated * gain_local
    gate_act = jax.nn.silu(gate)
    product = ssd_out * gate_act
    row_sums = pair_sum(jnp.stack([jnp.sum(product * product, 1), jnp.sum(product * grad_hat, 1)]))
    gate_scale = lax.rsqrt(row_sums[0] / DI + epsilon)[:, None]
    inner_sum = row_sums[1][:, None]
    gated = product * gate_scale * gain_local
    grad_product = gate_scale * (grad_hat - product * gate_scale * gate_scale * (inner_sum / DI))
    grad_gate = grad_product * ssd_out * silu_slope(gate)
    outer_reduced = lax.psum_scatter(
        jnp.concatenate([dot_first(features, grad_gate), dot_first(cotangent, gated)], 1),
        "seq",
        scatter_dimension=0,
        tiled=True,
    )
    layer_output = layer_input + pair_sum(dot_last(gated, out_full))
    gated_gain_part = jnp.sum(grad_gated * product * gate_scale, 0)
    ssd_grad = (grad_product * gate_act).reshape(rows, heads, P_SIZE)
    skip_grad = jnp.sum(ssd_grad * head_values, (0, 2))
    weighted_grad = ssd_grad * entry_weight[..., None]
    enter_grad = jnp.einsum("ihp,in->hpn", weighted_grad, read_map, precision=high)
    out_grads = carried_in(block_decay, enter_grad, True)
    read_grad = jnp.einsum("ihp,hpn->in", weighted_grad, entries, precision=high)
    logs_grad = jnp.sum(ssd_grad * state_read, 2) * entry_weight
    mix_grad = jnp.einsum("ihp,jhp->hij", ssd_grad, scaled, precision=high)
    scaled_grad = jnp.einsum("hij,ihp->jhp", weighted, ssd_grad, precision=high)
    score_grad = jnp.sum(mix_grad * decay_mat, 0)
    read_grad = read_grad + matmul(score_grad, input_map)
    input_grad_map = dot_first(score_grad, read_map)
    decay_term = mix_grad * weighted
    logs_grad = logs_grad + (jnp.sum(decay_term, 2) - jnp.sum(decay_term, 1)).T
    from_state = jnp.einsum("hpn,jn->jhp", out_grads, input_map, precision=high)
    scaled_grad = scaled_grad + tail_weight[..., None] * from_state
    input_grad_map = input_grad_map + jnp.einsum(
        "hpn,jhp->jn", out_grads, tail_scaled, precision=high
    )
    tail_grad = jnp.sum(from_state * tail_scaled, 2)
    last_grad = jnp.sum(tail_grad, 0) + jnp.sum(out_grads * entries, (1, 2)) * block_decay
    logs_grad = logs_grad - tail_grad
    decay_log_grad = jnp.flip(jnp.cumsum(jnp.flip(logs_grad, 0), 0), 0) + last_grad[None]
    grad_values = ssd_grad * skip[None, :, None] + scaled_grad * step_size[..., None]
    step_grad = jnp.sum(scaled_grad * head_values, 2) + decay_log_grad * rate
    rate_grad = jnp.sum(decay_log_grad * step_size, 0)
    log_rate_grad = rate_grad * rate
    step_pre_grad = step_grad * jax.nn.sigmoid(step_pre)
    bias_grad = jnp.sum(step_pre_grad, 0)
    step_full = lax.dynamic_update_slice_in_dim(
        jnp.zeros((rows, H), jnp.float32), step_pre_grad, head_start, 1
    )
    shared = pair_sum(jnp.concatenate([input_grad_map, read_grad, step_full], 1))
    act_grad = jnp.concatenate([grad_values.reshape(rows, inner), shared[:, : 2 * N]], 1)
    pre_grad = act_grad * silu_slope(conv_pre)
    conv_rows = []
    padded_grad = jnp.zeros_like(padded)
    for lag in range(K):
        masked = keeps[lag][:, None] * pre_grad
        conv_rows.append(jnp.sum(masked * padded[rim - lag : rim - lag + rows], 0))
        padded_grad = padded_grad + jnp.pad(masked * conv_local[lag], ((rim - lag, lag), (0, 0)))
    conv_rows.append(jnp.sum(pre_grad, 0))
    conv_local_grad = jnp.stack(conv_rows)
    spill = passed_along(padded_grad[:rim], "seq", -1)
    mixed_grad = padded_grad[rim:] + jnp.pad(spill, ((rows - rim, 0), (0, 0)))
    raw_grad = jnp.concatenate([mixed_grad, shared[:, 2 * N :]], 1)
    mixed_reduced = lax.psum_scatter(
        dot_first(features, raw_grad), "seq", scatter_dimension=0, tiled=True
    )
    once = jnp.where(jnp.arange(raw_grad.shape[1]) < inner, 1.0, 1.0 / model_count)
    features_grad = pair_sum(
        dot_last(grad_gate, gate_full) + dot_last(raw_grad * once, mixed_full)
    )
    norm_gain_part = jnp.sum(features_grad * normed, 0)
    gain_grad_in = features_grad * norm_gain
    input_grad = cotangent + scale * (
        gain_grad_in - normed * jnp.mean(gain_grad_in * normed, 1, keepdims=True)
    )

    factor = matrix_rate * 0.2 * D**0.5
    gate_weight_grad = outer_reduced[:, :inner]
    out_weight_grad = outer_reduced[:, inner:]
    new_gate_velocity, gate_update = matrix_momentum(gate_weight_grad, gate_weight_velocity)
    new_out_velocity, out_update = matrix_momentum(out_weight_grad, out_weight_velocity)
    outer_update = jnp.concatenate([gate_update, out_update], 1)
    outer_grams = padded_to(head_grams(outer_update), seq_count)
    per = outer_grams.shape[0] // seq_count
    outer_own = jnp.sum(exchange(outer_grams).reshape(seq_count, per, P_SIZE, P_SIZE), 0)
    outer_own = chain(outer_own)
    outer_poly = exchange(
        jnp.broadcast_to(outer_own[None], (seq_count,) + outer_own.shape).reshape(
            outer_grams.shape
        )
    )[: 2 * heads]
    outer_orth = apply_heads(outer_update, outer_poly)
    new_gate_weight = gate_weight - factor * outer_orth[:, :inner]
    new_out_weight = out_weight - factor * outer_orth[:, inner:]

    value_weight_grad = mixed_reduced[:, :inner]
    state_weight_grad = mixed_reduced[:, inner:]
    new_value_velocity, value_update = matrix_momentum(value_weight_grad, value_weight_velocity)
    new_state_velocity, state_update = matrix_momentum(state_weight_grad, state_weight_velocity)
    value_grams = padded_to(head_grams(value_update), seq_count)
    per = value_grams.shape[0] // seq_count
    value_rows = per * P_SIZE * P_SIZE // LANES
    map_update = state_update[:, : 2 * N].reshape(-1, 2, N)
    step_update = state_update[:, 2 * N :]
    map_grams = jnp.einsum("rup,ruq->upq", map_update, map_update, precision=highest)
    step_gram = lax.dot_general(
        step_update, step_update, (((0,), (0,)), ((), ())), precision=highest
    )
    small = jnp.concatenate(
        [
            map_grams.reshape(2 * N, N),
            jnp.pad(step_gram, ((0, 0), (0, N - H))),
            norm_gain_part.reshape(-1, LANES),
            conv_local_grad.reshape(-1, LANES),
            gated_gain_part.reshape(-1, LANES),
            jnp.pad(jnp.stack([bias_grad, log_rate_grad, skip_grad]), ((0, 0), (0, LANES - heads))),
        ],
        0,
    )
    small = padded_to(small, 8 * seq_count)
    small_rows = small.shape[0] // seq_count
    summed = jnp.sum(
        exchange(
            jnp.concatenate(
                [
                    value_grams.reshape(seq_count, value_rows, LANES),
                    small.reshape(seq_count, small_rows, LANES),
                ],
                1,
            )
        ),
        0,
    )
    value_own = chain(summed[:value_rows].reshape(per, P_SIZE, P_SIZE))
    told = jnp.concatenate([value_own.reshape(value_rows, LANES), summed[value_rows:]], 0)
    told = exchange(jnp.broadcast_to(told[None], (seq_count,) + told.shape))
    value_poly = told[:, :value_rows].reshape(seq_count * per, P_SIZE, P_SIZE)[:heads]
    small = told[:, value_rows:].reshape(seq_count * small_rows, LANES)
    state_poly = chain(
        jnp.stack(
            [small[:N], small[N : 2 * N], jnp.pad(small[2 * N : 2 * N + H], ((0, N - H), (0, 0)))]
        )
    )
    value_orth = apply_heads(value_update, value_poly)
    state_orth = jnp.concatenate(
        [
            jnp.einsum("rup,upq->ruq", map_update, state_poly[:2], precision=highest).reshape(
                -1, 2 * N
            ),
            jnp.dot(step_update, state_poly[2, :H, :H], precision=highest),
        ],
        1,
    )
    new_value_weight = value_weight - factor * value_orth
    new_state_weight = state_weight - factor * state_orth

    vectors = small[2 * N + H :]
    at = D // LANES
    norm_gain_grad = vectors[:at].reshape(D)
    other = swapped(vectors)
    first = jnp.where(model_index == 0, vectors, other)
    second = jnp.where(model_index == 0, other, vectors)
    conv_rows = (K + 1) * (inner + 2 * N) // LANES
    conv_first, conv_second = (
        side[at : at + conv_rows].reshape(K + 1, inner + 2 * N) for side in (first, second)
    )
    conv_value_grad = jnp.concatenate([conv_first[:, :inner], conv_second[:, :inner]], 1)
    conv_state_grad = conv_first[:, inner:]
    at = at + conv_rows
    gated_rows = inner // LANES
    gated_gain_grad = jnp.concatenate(
        [first[at : at + gated_rows].reshape(inner), second[at : at + gated_rows].reshape(inner)]
    )
    at = at + gated_rows
    head_params_grad = jnp.concatenate(
        [first[at : at + 3, :heads], second[at : at + 3, :heads]], 1
    )
    new_norm_gain, new_norm_velocity = vector_step(norm_gain, norm_gain_grad, norm_gain_velocity)
    new_conv_value, new_conv_value_velocity = vector_step(
        conv_value, conv_value_grad, conv_value_velocity
    )
    new_conv_state, new_conv_state_velocity = vector_step(
        conv_state, conv_state_grad, conv_state_velocity
    )
    new_head_params, new_head_velocity = vector_step(
        head_params, head_params_grad, head_params_velocity
    )
    new_gated_gain, new_gated_velocity = vector_step(
        gated_gain, gated_gain_grad, gated_gain_velocity
    )
    return (
        layer_output,
        input_grad,
        norm_gain_grad,
        gate_weight_grad,
        value_weight_grad,
        state_weight_grad,
        conv_value_grad,
        conv_state_grad,
        head_params_grad,
        gated_gain_grad,
        out_weight_grad,
        new_norm_gain,
        new_gate_weight,
        new_value_weight,
        new_state_weight,
        new_conv_value,
        new_conv_state,
        new_head_params,
        new_gated_gain,
        new_out_weight,
        new_norm_velocity,
        new_gate_velocity,
        new_value_velocity,
        new_state_velocity,
        new_conv_value_velocity,
        new_conv_state_velocity,
        new_head_velocity,
        new_gated_velocity,
        new_out_velocity,
    )


def solution(mesh):
    return jax.shard_map(
        body,
        mesh=mesh,
        in_specs=(
            P("seq", None),
            P("seq", None),
            P("seq"),
            P(),
            P("seq", "mp"),
            P("seq", "mp"),
            P("seq", None),
            P(),
            P(),
            P(),
            P(),
            P("seq", "mp"),
            P(),
            P("seq", "mp"),
            P("seq", "mp"),
            P("seq", None),
            P(),
            P(),
            P(),
            P(),
            P("seq", "mp"),
        ),
        out_specs=(
            P("seq", None),
            P("seq", None),
            P(),
            P("seq", "mp"),
            P("seq", "mp"),
            P("seq", None),
            P(),
            P(),
            P(),
            P(),
            P("seq", "mp"),
            P(),
            P("seq", "mp"),
            P("seq", "mp"),
            P("seq", None),
            P(),
            P(),
            P(),
            P(),
            P("seq", "mp"),
            P(),
            P("seq", "mp"),
            P("seq", "mp"),
            P("seq", None),
            P(),
            P(),
            P(),
            P(),
            P("seq", "mp"),
        ),
        check_vma=False,
    )
```

time: 1670 us -> 743 us (0.44)
  waiting for transfers between devices: 835 us -> 377 us
  blocking collectives: 459 us -> 58.4 us
  matrix products: 167 us -> 92.4 us
  local copies, waits for them, and re-layouts: 82.2 us -> 41.6 us
  starting transfers between devices: 12.4 us -> 45.6 us
  Pallas kernels: 0 us -> 18.1 us
    psum x8 -> x0, blocking collectives: 418 us -> none  [the longest x5 369 us: body(): grams = lax.psum(gram_of(current), 'seq')]
    psum x8 -> x0, waiting for transfers between devices: 272 us -> none  [the longest x5 264 us: body(): grams = lax.psum(gram_of(current), 'seq')]
    all_gather x6 -> x2, waiting for transfers between devices: 391 us -> 123 us  [the longest x1 82.4 us: body(): lax.all_gather(jnp.concatenate([value_weight, state_weight], 1), 'seq', a...]
    dot_general x67 -> x29, matrix products: 167 us -> 92.4 us  [the longest x4 21.1 us: dot_last(): lax.dot_general(left, right, (((1,), (1,)), ((), ())), precision=high)]
    all_to_all x0 -> x2, blocking collectives: none -> 58.4 us  [exchange(): return lax.all_to_all(array, 'seq', 0, 0, tiled=True)]
    all_to_all x0 -> x6, waiting for transfers between devices: none -> 46.4 us  [exchange(): return lax.all_to_all(array, 'seq', 0, 0, tiled=True)]
    all_gather x1 -> x0, blocking collectives: 41.1 us -> none  [carried_in(): gathered = jax.tree.map(lambda a: lax.all_gather(a, axis), part)]
    reduce_scatter x1 -> x2, waiting for transfers between devices: 166 us -> 204 us  [the longest x1 108 us: body(): lax.psum_scatter(jnp.concatenate([dot_first(features, grad_gate), dot_fir...]
  transfers between devices with their start and end apart: 18 -> 18, of which waited for: 13 -> 13; matrix products, arithmetic and copies ran while one was open for 10% -> 17% of each run, Pallas kernels for 0% -> 2%
where the time goes in v1:
time: 743 us; the launch traced here: 734 us
  waiting for transfers between devices  377 us (51%)
  matrix products  92.4 us (12%)
  other arithmetic  77 us (10%)
  blocking collectives  58.4 us (8%)
  starting transfers between devices  45.6 us (6%)
  local copies, waits for them, and re-layouts  41.6 us (6%)
  between operations  23.6 us (3%)
  Pallas kernels  18.1 us (2%)
    reduce_scatter x1, waiting for transfers between devices, body(): lax.psum_scatter(jnp.concatenate([dot_first(features, grad_gate), dot_fir...  108 us
    reduce_scatter x1, waiting for transfers between devices, body(): lax.psum_scatter(dot_first(features, raw_grad), 'seq', scatter_dimension=...  96.2 us
    all_gather x1, waiting for transfers between devices, body(): lax.all_gather(jnp.concatenate([value_weight, state_weight], 1), 'seq', a...  82.4 us
    all_to_all x2, blocking collectives, exchange(): return lax.all_to_all(array, 'seq', 0, 0, tiled=True)  58.4 us
    all_to_all x6, waiting for transfers between devices, exchange(): return lax.all_to_all(array, 'seq', 0, 0, tiled=True)  46.4 us
    all_gather x1, waiting for transfers between devices, body(): lax.all_gather(jnp.concatenate([gate_weight, out_weight], 1), 'seq', axis...  40.2 us
    all_to_all x6, starting transfers between devices, exchange(): return lax.all_to_all(array, 'seq', 0, 0, tiled=True)  34.9 us
    dot_general x4, matrix products, dot_last(): lax.dot_general(left, right, (((1,), (1,)), ((), ())), precision=high)  21.1 us
  transfers between devices with their start and end apart: 18, of which 13 were waited for; matrix products, arithmetic and copies ran while one was open for 17% of the time, Pallas kernels for 2%

profile of v1, /device:TPU:0, one launch (start us, length us, event | category | flops | bytes accessed | tf_op | source)
XLA Modules:
  0.0 733.9 jit_solution(12822940114228937102)
XLA Ops:
  20.4 82.4 %all-gather.3.cloned.1.call-done = f32[1024,1312]{1,0:T(8,128)} async-done(((f32[64,1312]{1,0:T(8,128)}), f32[1024,1312]{1,0:T(8,128)}) %all-gather.3.cloned.1.call-update) | async-done | bytes 5373968 | tf_op jit(solution)/shard_map/all_gather | solution.py:196
  102.8 7.3 fusion.78
  118.2 6.1 fusion.51
  126.4 36.8 %all_to_all.40.part_ref = f32[16,72,128]{2,1,0:T(8,128)} all-to-all(f32[16,72,128]{2,1,0:T(8,128)S(1)} %pad_maximum_fusion.6), channel_id=1, replica_groups=mesh['seq'=16,'mp'=2] {'seq'}, dimensions={0} | all-to-all | bytes 1179648 | tf_op jit(solution)/shard_map/all_to_all | solution.py:45
  173.5 8.1 %all-to-all-done.1 = f32[16,64,128]{2,1,0:T(8,128)} async-done(((f32[16,64,128]{2,1,0:T(8,128)}), f32[16,64,128]{2,1,0:T(8,128)}, u32[]{:S(2)}, u32[]{:S(2)}) %all-to-all-start.1) | async-done | bytes 524320 | tf_op jit(solution)/shard_map/all_to_all | solution.py:45
  188.1 40.2 %all-gather.5.cloned.1.call-done = f32[1024,2048]{1,0:T(8,128)} async-done(((f32[64,2048]{1,0:T(8,128)}), f32[1024,2048]{1,0:T(8,128)}) %all-gather.5.cloned.1.call-update) | async-done | bytes 8388624 | tf_op jit(solution)/shard_map/all_gather | solution.py:199
  228.3 5.8 fusion.12
  234.1 5.9 multiply_reduce_fusion.12
  245.1 21.6 %all_to_all.41.part_ref = f32[16,72,128]{2,1,0:T(8,128)} all-to-all(f32[16,72,128]{2,1,0:T(8,128)S(1)} %pad_maximum_fusion.5), channel_id=1, replica_groups=mesh['seq'=16,'mp'=2] {'seq'}, dimensions={0} | all-to-all | bytes 1179648 | tf_op jit(solution)/shard_map/all_to_all | solution.py:45
  273.2 6.2 fusion.14
  289.1 5.1 fusion.110
  337.3 7.1 fusion.52
  355.9 7.5 %fusion.38 = f32[256,1024]{1,0:T(8,128)S(1)} fusion(f32[1024,1312]{1,0:T(8,128)} %all-gather.3.cloned.1.call-done, f32[256,32]{0,1:T(8,128)S(1)} %slice.314, f32[256,1280]{0,1:T(8,128)S(1)} %slice_add_fusion, f32[1312]{0:T(1024)S(1)} %fusion.138), kind=kOutput, calls=%fused_computation.38 | convolution fusion | flops 2064269312 | bytes 7771264 | tf_op jit(solution)/shard_map/dot_general | solution.py:53
  363.4 5.7 fusion.32
  374.2 96.2 %reduce-scatter.3.cloned.1.call-done = f32[64,1312]{1,0:T(8,128)} async-done(((f32[1024,1312]{1,0:T(8,128)}), f32[64,1312]{1,0:T(8,128)}) %reduce-scatter.3.cloned.1.call-update) | async-done | bytes 335888 | tf_op jit(solution)/shard_map/reduce_scatter | solution.py:329
  484.0 7.5 %all-to-all-start.4 = ((f32[16,56,128]{2,1,0:T(8,128)}), f32[16,56,128]{2,1,0:T(8,128)}, u32[]{:S(2)}, u32[]{:S(2)}) async-start(f32[16,56,128]{2,1,0:T(8,128)} %pad_maximum_fusion.9), calls=%async_computation.5 | async-start | bytes 917504 | tf_op jit(solution)/shard_map/all_to_all | solution.py:45
  491.5 6.9 fusion.6
  513.5 7.2 all-to-all-start.5
  526.9 11.3 %all-to-all-done.5 = f32[16,56,128]{2,1,0:T(8,128)} async-done(((f32[16,56,128]{2,1,0:T(8,128)}), f32[16,56,128]{2,1,0:T(8,128)}, u32[]{:S(2)}, u32[]{:S(2)}) %all-to-all-start.5) | async-done | bytes 458784 | tf_op jit(solution)/shard_map/all_to_all | solution.py:45
  543.2 5.7 chain.5
  554.4 107.7 %reduce-scatter.5.cloned.1.call-done = f32[64,2048]{1,0:T(8,128)} async-done(((f32[1024,2048]{1,0:T(8,128)}), f32[64,2048]{1,0:T(8,128)}) %reduce-scatter.5.cloned.1.call-update) | async-done | bytes 524304 | tf_op jit(solution)/shard_map/reduce_scatter | solution.py:275
  669.0 7.5 %all-to-all-start.6 = ((f32[16,1,8192]{2,1,0:T(1,128)}), f32[16,1,8192]{2,1,0:T(1,128)S(1)}, u32[]{:S(2)}, u32[]{:S(2)}) async-start(f32[16,1,8192]{2,1,0:T(1,128)} %reshape.399), calls=%async_computation.8 | async-start | bytes 1048576 | tf_op jit(solution)/shard_map/all_to_all | solution.py:45
  679.8 11.5 %all-to-all-done.6 = f32[16,1,8192]{2,1,0:T(1,128)S(1)} async-done(((f32[16,1,8192]{2,1,0:T(1,128)}), f32[16,1,8192]{2,1,0:T(1,128)S(1)}, u32[]{:S(2)}, u32[]{:S(2)}) %all-to-all-start.6) | async-done | bytes 524320 | tf_op jit(solution)/shard_map/all_to_all | solution.py:45
  710.5 9.8 %all-to-all-done.7 = f32[16,1,8192]{2,1,0:T(1,128)S(1)} async-done(((f32[16,1,8192]{2,1,0:T(1,128)}), f32[16,1,8192]{2,1,0:T(1,128)S(1)}, u32[]{:S(2)}, u32[]{:S(2)}) %all-to-all-start.7) | async-done | bytes 524320 | tf_op jit(solution)/shard_map/all_to_all | solution.py:45
  (439 shorter events, 193.1 us)
Async XLA Ops:
  7.3 95.6 %all-gather.3.cloned.1.call-start = ((), (), s32[]{:S(2)}) async-start(), calls=%async_computation.10 | async-start | bytes 6127616 | tf_op jit(solution)/shard_map/all_gather | solution.py:196
  9.2 219.1 %all-gather.5.cloned.1.call-start = ((), (), s32[]{:S(2)}) async-start(), calls=%async_computation.11 | async-start | bytes 8912896 | tf_op jit(solution)/shard_map/all_gather | solution.py:199
  11.2 8.3 %collective-permute-start = (f32[3]{0:T(128)S(1)}, f32[3]{0:T(128)S(1)}, u32[]{:S(2)}, u32[]{:S(2)}) collective-permute-start(f32[3]{0:T(128)S(1)} %slice.230), channel_id=1, source_target_pairs={{0,2},{2,4},{4,6},{6,8},{8,10},{10,12},{12,14},{14,16},{16,18},{18... | collective-permute-start | bytes 44 | tf_op jit(solution)/shard_map/ppermute | solution.py:33
  18.1 100.0 %copy-start.51 = (f32[1280]{0:T(1024)}, f32[1280]{0:T(1024)S(1)}, u32[]{:S(2)}) copy-start(f32[1280]{0:T(1024)S(1)} %get-tuple-element.46) | copy-start | bytes 15364
  18.1 100.0 %copy-start.53 = (f32[1280]{0:T(1024)}, f32[1280]{0:T(1024)S(1)}, u32[]{:S(2)}) copy-start(f32[1280]{0:T(1024)S(1)} %get-tuple-element.47) | copy-start | bytes 15364
  112.4 5.4 collective-permute-start.1
  165.1 16.4 %all-to-all-start.1 = ((f32[16,64,128]{2,1,0:T(8,128)}), f32[16,64,128]{2,1,0:T(8,128)}, u32[]{:S(2)}, u32[]{:S(2)}) async-start(f32[16,64,128]{2,1,0:T(8,128)} %carry.2), calls=%async_computation.1 | async-start | bytes 1048576 | tf_op jit(solution)/shard_map/all_to_all | solution.py:45
  240.0 1.2 collective-permute-start.2
  268.7 18.5 %all-to-all-start.3 = ((f32[16,64,128]{2,1,0:T(8,128)}), f32[16,64,128]{2,1,0:T(8,128)}, u32[]{:S(2)}, u32[]{:S(2)}) async-start(f32[16,64,128]{2,1,0:T(8,128)} %carry.3), calls=%async_computation.3 | async-start | bytes 1048576 | tf_op jit(solution)/shard_map/all_to_all | solution.py:45
  272.9 197.5 %reduce-scatter.3.cloned.1.call-start = ((), (), s32[]{:S(2)}) async-start(), calls=%async_computation.12 | async-start | bytes 6127616 | tf_op jit(solution)/shard_map/reduce_scatter | solution.py:329
  314.4 1.6 collective-permute-start.4
  326.5 7.5 %collective-permute-start.5 = (f32[3,1280]{1,0:T(4,128)S(1)}, f32[3,1280]{1,0:T(4,128)S(1)}, u32[]{:S(2)}, u32[]{:S(2)}) collective-permute-start(f32[3,1280]{1,0:T(4,128)S(1)} %copy.268), channel_id=1, source_target_pairs={{2,0},{4,2},{6,4},{8,6},{10,8},{12,10},{14,12},{16,14},{18,16},{20... | collective-permute-start | bytes 46088 | tf_op jit(solution)/shard_map/ppermute | solution.py:33
  344.4 317.7 %reduce-scatter.5.cloned.1.call-start = ((), (), s32[]{:S(2)}) async-start(), calls=%async_computation.13 | async-start | bytes 8912896 | tf_op jit(solution)/shard_map/reduce_scatter | solution.py:275
  369.1 2.9 collective-permute-start.6
  370.4 100.0 %copy-start.50 = (f32[64,288]{1,0:T(8,128)S(1)}, f32[64,288]{1,0:T(8,128)}, u32[]{:S(2)}) copy-start(f32[64,288]{1,0:T(8,128)} %param.36) | copy-start | bytes 221188
  370.4 102.9 %copy-start.79 = (f32[1024]{0:T(1024)S(1)}, f32[1024]{0:T(1024)}, u32[]{:S(2)}) copy-start(f32[1024]{0:T(1024)} %get-tuple-element.89) | copy-start | bytes 12292
  484.0 22.2 %all-to-all-start.4 = ((f32[16,56,128]{2,1,0:T(8,128)}), f32[16,56,128]{2,1,0:T(8,128)}, u32[]{:S(2)}, u32[]{:S(2)}) async-start(f32[16,56,128]{2,1,0:T(8,128)} %pad_maximum_fusion.9), calls=%async_computation.5 | async-start | bytes 917504 | tf_op jit(solution)/shard_map/all_to_all | solution.py:45
  498.4 25.0 %collective-permute-start.3 = (f32[256,1024]{1,0:T(8,128)}, f32[256,1024]{1,0:T(8,128)}, u32[]{:S(2)}, u32[]{:S(2)}) collective-permute-start(f32[256,1024]{1,0:T(8,128)} %fusion.6), channel_id=1, source_target_pairs={{0,1},{1,0},{2,3},{3,2},{4,5},{5,4},{6,7},{7,6},{8,9},{9,8},{10,11... | collective-permute-start | bytes 3145736 | tf_op jit(solution)/shard_map/ppermute | solution.py:37
  513.5 24.7 %all-to-all-start.5 = ((f32[16,56,128]{2,1,0:T(8,128)}), f32[16,56,128]{2,1,0:T(8,128)}, u32[]{:S(2)}, u32[]{:S(2)}) async-start(f32[16,56,128]{2,1,0:T(8,128)} %broadcast_in_dim.36), calls=%async_computation.6 | async-start | bytes 917504 | tf_op jit(solution)/shard_map/all_to_all | solution.py:45
  539.0 15.3 %collective-permute-start.7 = (f32[96,128]{1,0:T(8,128)S(1)}, f32[96,128]{1,0:T(8,128)S(1)}, u32[]{:S(2)}, u32[]{:S(2)}) collective-permute-start(f32[96,128]{1,0:T(8,128)S(1)} %bitcast.204), channel_id=1, source_target_pairs={{0,1},{1,0},{2,3},{3,2},{4,5},{5,4},{6,7},{7,6},{8,9},{9,8},{10,11... | collective-permute-start | bytes 147464 | tf_op jit(solution)/shard_map/ppermute | solution.py:37
  551.7 110.4 %copy-start.40 = (f32[64,1024]{1,0:T(8,128)S(1)}, f32[64,1024]{1,0:T(8,128)}, u32[]{:S(2)}) copy-start(f32[64,1024]{1,0:T(8,128)} %param.41) | copy-start | bytes 786436
  551.7 110.4 %copy-start.41 = (f32[64,1024]{1,0:T(8,128)S(1)}, f32[64,1024]{1,0:T(8,128)}, u32[]{:S(2)}) copy-start(f32[64,1024]{1,0:T(8,128)} %param.34) | copy-start | bytes 786436
  669.0 22.3 %all-to-all-start.6 = ((f32[16,1,8192]{2,1,0:T(1,128)}), f32[16,1,8192]{2,1,0:T(1,128)S(1)}, u32[]{:S(2)}, u32[]{:S(2)}) async-start(f32[16,1,8192]{2,1,0:T(1,128)} %reshape.399), calls=%async_computation.8 | async-start | bytes 1048576 | tf_op jit(solution)/shard_map/all_to_all | solution.py:45
  701.9 18.4 %all-to-all-start.7 = ((f32[16,1,8192]{2,1,0:T(1,128)}), f32[16,1,8192]{2,1,0:T(1,128)S(1)}, u32[]{:S(2)}, u32[]{:S(2)}) async-start(f32[16,1,8192]{2,1,0:T(1,128)} %reshape.401), calls=%async_computation.9 | async-start | bytes 1048576 | tf_op jit(solution)/shard_map/all_to_all | solution.py:45
  (104 other events, 1804.4 us)
Sparse Core Ops, SparseCore 0:
  11.3 91.4 all-gather.2
  105.6 122.5 all-gather.4
  344.6 125.7 reduce-scatter.2
  472.6 189.4 reduce-scatter.4

commit v2 on v1

--- a/solution.py
+++ b/solution.py
@@ -135,6 +135,14 @@
     return jnp.pad(array, ((0, extra),) + ((0, 0),) * (array.ndim - 1))
 
 
+def scatter_ready(parts):
+    width = sum(part.shape[1] for part in parts)
+    extra = -width % 96
+    if extra:
+        parts = parts + [jnp.zeros((parts[0].shape[0], extra), jnp.float32)]
+    return jnp.concatenate(parts, 1)
+
+
 def head_grams(update):
     split = update.reshape(update.shape[0], -1, P_SIZE)
     return jnp.einsum("rup,ruq->upq", split, split, precision=highest)
@@ -143,6 +151,26 @@
 def apply_heads(update, polynomials):
     split = update.reshape(update.shape[0], -1, P_SIZE)
     return jnp.einsum("rup,upq->ruq", split, polynomials, precision=highest).reshape(update.shape)
+
+
+def gathered_sum(grams, others):
+    count = lax.axis_size("seq")
+    others = padded_to(others, 8 * count)
+    own_rows = others.shape[0] // count
+    sent = jnp.concatenate(
+        [grams.reshape(count, -1, LANES), others.reshape(count, own_rows, LANES)], 1
+    )
+    return jnp.sum(exchange(sent), 0), own_rows
+
+
+def told_all(own, others, gram_rows, other_rows):
+    count = lax.axis_size("seq")
+    told = jnp.concatenate([own.reshape(gram_rows, LANES), others], 0)
+    told = exchange(jnp.broadcast_to(told[None], (count,) + told.shape))
+    return (
+        told[:, :gram_rows].reshape(-1, P_SIZE, P_SIZE),
+        told[:, gram_rows:].reshape(count * other_rows, LANES),
+    )
 
 
 def vector_step(current, gradient, velocity):
@@ -193,23 +221,30 @@
     inner_start = model_index * inner
     head_start = model_index * heads
     rim = K - 1
+    own_columns = inner + N + heads
+    own_map = lax.dynamic_slice_in_dim(state_weight, model_index * N, N, 1)
+    own_step = lax.dynamic_slice_in_dim(state_weight, 2 * N + head_start, heads, 1)
     mixed_full = lax.all_gather(
-        jnp.concatenate([value_weight, state_weight], 1), "seq", axis=0, tiled=True
+        jnp.concatenate([value_weight, own_map, own_step], 1), "seq", axis=0, tiled=True
     )
     outer_full = lax.all_gather(
         jnp.concatenate([gate_weight, out_weight], 1), "seq", axis=0, tiled=True
     )
     gain_local = lax.dynamic_slice_in_dim(gated_gain, inner_start, inner, 0)
     conv_local = jnp.concatenate(
-        [lax.dynamic_slice_in_dim(conv_value, inner_start, inner, 1), conv_state], 1
+        [
+            lax.dynamic_slice_in_dim(conv_value, inner_start, inner, 1),
+            lax.dynamic_slice_in_dim(conv_state, model_index * N, N, 1),
+        ],
+        1,
     )
     head_local = lax.dynamic_slice_in_dim(head_params, head_start, heads, 1)
     starts_float = doc_starts.astype(jnp.float32)
     scale = lax.rsqrt(jnp.mean(layer_input * layer_input, 1, keepdims=True) + epsilon)
     normed = layer_input * scale
     features = normed * norm_gain
-    raw = matmul(features, mixed_full)
-    mixed_in = raw[:, : inner + 2 * N]
+    raw = jnp.dot(features, mixed_full, precision=highest)
+    mixed_in = raw[:, : inner + N]
     prev_starts = passed_along(starts_float[rows - rim :], "seq", 1)
     prev_rows = passed_along(mixed_in[rows - rim :], "seq", 1)
     padded = jnp.concatenate([prev_rows, mixed_in], 0)
@@ -226,11 +261,11 @@
         )
     activated = jax.nn.silu(conv_pre)
     head_values = activated[:, :inner].reshape(rows, heads, P_SIZE)
-    input_map = activated[:, inner : inner + N]
-    read_map = activated[:, inner + N :]
-    step_pre = (
-        lax.dynamic_slice_in_dim(raw, inner + 2 * N + head_start, heads, 1) + head_local[0]
-    )
+    this_map = activated[:, inner:]
+    other_map = swapped(this_map)
+    input_map = jnp.where(model_index == 0, this_map, other_map)
+    read_map = jnp.where(model_index == 0, other_map, this_map)
+    step_pre = raw[:, inner + N :] + head_local[0]
     step_size = jax.nn.softplus(step_pre)
     rate = -jnp.exp(head_local[1])
     skip = head_local[2]
@@ -243,19 +278,19 @@
     head_logs = log_sums.T
     log_gap = head_logs[:, :, None] - head_logs[:, None, :]
     decay_mat = jnp.where(causal_mask, jnp.exp(jnp.where(causal_mask, log_gap, 0.0)), 0.0)
-    scores = dot_last(read_map, input_map)
+    scores = lax.dot_general(read_map, input_map, (((1,), (1,)), ((), ())), precision=highest)
     weighted = decay_mat * scores[None]
     scaled = head_values * step_size[..., None]
     last_log = log_sums[-1]
     last_segment = segment[-1]
     tail_weight = jnp.exp(last_log[None] - log_sums) * (segment == last_segment)[:, None]
     tail_scaled = scaled * tail_weight[..., None]
-    block_state = jnp.einsum("jhp,jn->hpn", tail_scaled, input_map, precision=high)
+    block_state = jnp.einsum("jhp,jn->hpn", tail_scaled, input_map, precision=highest)
     block_decay = jnp.exp(last_log) * (last_segment == 0)
     entry_weight = jnp.exp(log_sums) * (segment == 0)[:, None]
     entries = carried_in(block_decay, block_state, False)
-    intra = jnp.einsum("hij,jhp->ihp", weighted, scaled, precision=high)
-    state_read = jnp.einsum("hpn,in->ihp", entries, read_map, precision=high)
+    intra = jnp.einsum("hij,jhp->ihp", weighted, scaled, precision=highest)
+    state_read = jnp.einsum("hpn,in->ihp", entries, read_map, precision=highest)
     ssd_out = (
         intra + entry_weight[..., None] * state_read + head_values * skip[None, :, None]
     ).reshape(rows, inner)
@@ -272,32 +307,31 @@
     gated = product * gate_scale * gain_local
     grad_product = gate_scale * (grad_hat - product * gate_scale * gate_scale * (inner_sum / DI))
     grad_gate = grad_product * ssd_out * silu_slope(gate)
-    outer_reduced = lax.psum_scatter(
-        jnp.concatenate([dot_first(features, grad_gate), dot_first(cotangent, gated)], 1),
-        "seq",
-        scatter_dimension=0,
-        tiled=True,
-    )
+    outer_partial = scatter_ready([dot_first(features, grad_gate), dot_first(cotangent, gated)])
+    outer_partial, grad_product = lax.optimization_barrier((outer_partial, grad_product))
+    outer_reduced = lax.psum_scatter(outer_partial, "seq", scatter_dimension=0, tiled=True)
     layer_output = layer_input + pair_sum(dot_last(gated, out_full))
     gated_gain_part = jnp.sum(grad_gated * product * gate_scale, 0)
     ssd_grad = (grad_product * gate_act).reshape(rows, heads, P_SIZE)
     skip_grad = jnp.sum(ssd_grad * head_values, (0, 2))
     weighted_grad = ssd_grad * entry_weight[..., None]
-    enter_grad = jnp.einsum("ihp,in->hpn", weighted_grad, read_map, precision=high)
+    enter_grad = jnp.einsum("ihp,in->hpn", weighted_grad, read_map, precision=highest)
     out_grads = carried_in(block_decay, enter_grad, True)
-    read_grad = jnp.einsum("ihp,hpn->in", weighted_grad, entries, precision=high)
+    read_grad = jnp.einsum("ihp,hpn->in", weighted_grad, entries, precision=highest)
     logs_grad = jnp.sum(ssd_grad * state_read, 2) * entry_weight
-    mix_grad = jnp.einsum("ihp,jhp->hij", ssd_grad, scaled, precision=high)
-    scaled_grad = jnp.einsum("hij,ihp->jhp", weighted, ssd_grad, precision=high)
+    mix_grad = jnp.einsum("ihp,jhp->hij", ssd_grad, scaled, precision=highest)
+    scaled_grad = jnp.einsum("hij,ihp->jhp", weighted, ssd_grad, precision=highest)
     score_grad = jnp.sum(mix_grad * decay_mat, 0)
-    read_grad = read_grad + matmul(score_grad, input_map)
-    input_grad_map = dot_first(score_grad, read_map)
+    read_grad = read_grad + jnp.dot(score_grad, input_map, precision=highest)
+    input_grad_map = lax.dot_general(
+        score_grad, read_map, (((0,), (0,)), ((), ())), precision=highest
+    )
     decay_term = mix_grad * weighted
     logs_grad = logs_grad + (jnp.sum(decay_term, 2) - jnp.sum(decay_term, 1)).T
-    from_state = jnp.einsum("hpn,jn->jhp", out_grads, input_map, precision=high)
+    from_state = jnp.einsum("hpn,jn->jhp", out_grads, input_map, precision=highest)
     scaled_grad = scaled_grad + tail_weight[..., None] * from_state
     input_grad_map = input_grad_map + jnp.einsum(
-        "hpn,jhp->jn", out_grads, tail_scaled, precision=high
+        "hpn,jhp->jn", out_grads, tail_scaled, precision=highest
     )
     tail_grad = jnp.sum(from_state * tail_scaled, 2)
     last_grad = jnp.sum(tail_grad, 0) + jnp.sum(out_grads * entries, (1, 2)) * block_decay
@@ -309,11 +343,11 @@
     log_rate_grad = rate_grad * rate
     step_pre_grad = step_grad * jax.nn.sigmoid(step_pre)
     bias_grad = jnp.sum(step_pre_grad, 0)
-    step_full = lax.dynamic_update_slice_in_dim(
-        jnp.zeros((rows, H), jnp.float32), step_pre_grad, head_start, 1
-    )
-    shared = pair_sum(jnp.concatenate([input_grad_map, read_grad, step_full], 1))
-    act_grad = jnp.concatenate([grad_values.reshape(rows, inner), shared[:, : 2 * N]], 1)
+    this_grad = jnp.where(model_index == 0, input_grad_map, read_grad)
+    other_grad = jnp.where(model_index == 0, read_grad, input_grad_map)
+    act_grad = jnp.concatenate(
+        [grad_values.reshape(rows, inner), this_grad + swapped(other_grad)], 1
+    )
     pre_grad = act_grad * silu_slope(conv_pre)
     conv_rows = []
     padded_grad = jnp.zeros_like(padded)
@@ -325,14 +359,11 @@
     conv_local_grad = jnp.stack(conv_rows)
     spill = passed_along(padded_grad[:rim], "seq", -1)
     mixed_grad = padded_grad[rim:] + jnp.pad(spill, ((rows - rim, 0), (0, 0)))
-    raw_grad = jnp.concatenate([mixed_grad, shared[:, 2 * N :]], 1)
-    mixed_reduced = lax.psum_scatter(
-        dot_first(features, raw_grad), "seq", scatter_dimension=0, tiled=True
-    )
-    once = jnp.where(jnp.arange(raw_grad.shape[1]) < inner, 1.0, 1.0 / model_count)
-    features_grad = pair_sum(
-        dot_last(grad_gate, gate_full) + dot_last(raw_grad * once, mixed_full)
-    )
+    raw_grad = jnp.concatenate([mixed_grad, step_pre_grad], 1)
+    mixed_partial = scatter_ready([dot_first(features, raw_grad)])
+    mixed_partial, raw_grad = lax.optimization_barrier((mixed_partial, raw_grad))
+    mixed_reduced = lax.psum_scatter(mixed_partial, "seq", scatter_dimension=0, tiled=True)
+    features_grad = pair_sum(dot_last(grad_gate, gate_full) + dot_last(raw_grad, mixed_full))
     norm_gain_part = jnp.sum(features_grad * normed, 0)
     gain_grad_in = features_grad * norm_gain
     input_grad = cotangent + scale * (
@@ -341,25 +372,58 @@
 
     factor = matrix_rate * 0.2 * D**0.5
     gate_weight_grad = outer_reduced[:, :inner]
-    out_weight_grad = outer_reduced[:, inner:]
+    out_weight_grad = outer_reduced[:, inner : 2 * inner]
     new_gate_velocity, gate_update = matrix_momentum(gate_weight_grad, gate_weight_velocity)
     new_out_velocity, out_update = matrix_momentum(out_weight_grad, out_weight_velocity)
     outer_update = jnp.concatenate([gate_update, out_update], 1)
     outer_grams = padded_to(head_grams(outer_update), seq_count)
     per = outer_grams.shape[0] // seq_count
-    outer_own = jnp.sum(exchange(outer_grams).reshape(seq_count, per, P_SIZE, P_SIZE), 0)
-    outer_own = chain(outer_own)
-    outer_poly = exchange(
-        jnp.broadcast_to(outer_own[None], (seq_count,) + outer_own.shape).reshape(
-            outer_grams.shape
-        )
-    )[: 2 * heads]
-    outer_orth = apply_heads(outer_update, outer_poly)
+    outer_rows = per * P_SIZE * P_SIZE // LANES
+    vectors = jnp.concatenate(
+        [
+            norm_gain_part.reshape(-1, LANES),
+            conv_local_grad.reshape(-1, LANES),
+            gated_gain_part.reshape(-1, LANES),
+            jnp.pad(jnp.stack([bias_grad, log_rate_grad, skip_grad]), ((0, 0), (0, LANES - heads))),
+        ],
+        0,
+    )
+    summed, vector_rows = gathered_sum(outer_grams, vectors)
+    outer_own = chain(summed[:outer_rows].reshape(per, P_SIZE, P_SIZE))
+    outer_poly, vectors = told_all(outer_own, summed[outer_rows:], outer_rows, vector_rows)
+    outer_orth = apply_heads(outer_update, outer_poly[: 2 * heads])
     new_gate_weight = gate_weight - factor * outer_orth[:, :inner]
     new_out_weight = out_weight - factor * outer_orth[:, inner:]
 
+    at = D // LANES
+    norm_gain_grad = vectors[:at].reshape(D)
+    other = swapped(vectors)
+    first = jnp.where(model_index == 0, vectors, other)
+    second = jnp.where(model_index == 0, other, vectors)
+    conv_rows = (K + 1) * (inner + N) // LANES
+    conv_first, conv_second = (
+        side[at : at + conv_rows].reshape(K + 1, inner + N) for side in (first, second)
+    )
+    conv_value_grad = jnp.concatenate([conv_first[:, :inner], conv_second[:, :inner]], 1)
+    conv_state_grad = jnp.concatenate([conv_first[:, inner:], conv_second[:, inner:]], 1)
+    at = at + conv_rows
+    gated_rows = inner // LANES
+    gated_gain_grad = jnp.concatenate(
+        [first[at : at + gated_rows].reshape(inner), second[at : at + gated_rows].reshape(inner)]
+    )
+    at = at + gated_rows
+    head_params_grad = jnp.concatenate(
+        [first[at : at + 3, :heads], second[at : at + 3, :heads]], 1
+    )
+
     value_weight_grad = mixed_reduced[:, :inner]
-    state_weight_grad = mixed_reduced[:, inner:]
+    this_state = mixed_reduced[:, inner:own_columns]
+    other_state = swapped(this_state)
+    first = jnp.where(model_index == 0, this_state, other_state)
+    second = jnp.where(model_index == 0, other_state, this_state)
+    state_weight_grad = jnp.concatenate(
+        [first[:, :N], second[:, :N], first[:, N:], second[:, N:]], 1
+    )
     new_value_velocity, value_update = matrix_momentum(value_weight_grad, value_weight_velocity)
     new_state_velocity, state_update = matrix_momentum(state_weight_grad, state_weight_velocity)
     value_grams = padded_to(head_grams(value_update), seq_count)
@@ -372,41 +436,17 @@
         step_update, step_update, (((0,), (0,)), ((), ())), precision=highest
     )
     small = jnp.concatenate(
-        [
-            map_grams.reshape(2 * N, N),
-            jnp.pad(step_gram, ((0, 0), (0, N - H))),
-            norm_gain_part.reshape(-1, LANES),
-            conv_local_grad.reshape(-1, LANES),
-            gated_gain_part.reshape(-1, LANES),
-            jnp.pad(jnp.stack([bias_grad, log_rate_grad, skip_grad]), ((0, 0), (0, LANES - heads))),
-        ],
-        0,
-    )
-    small = padded_to(small, 8 * seq_count)
-    small_rows = small.shape[0] // seq_count
-    summed = jnp.sum(
-        exchange(
-            jnp.concatenate(
-                [
-                    value_grams.reshape(seq_count, value_rows, LANES),
-                    small.reshape(seq_count, small_rows, LANES),
-                ],
-                1,
-            )
-        ),
-        0,
-    )
+        [map_grams.reshape(2 * N, N), jnp.pad(step_gram, ((0, 0), (0, N - H)))], 0
+    )
+    summed, small_rows = gathered_sum(value_grams, small)
     value_own = chain(summed[:value_rows].reshape(per, P_SIZE, P_SIZE))
-    told = jnp.concatenate([value_own.reshape(value_rows, LANES), summed[value_rows:]], 0)
-    told = exchange(jnp.broadcast_to(told[None], (seq_count,) + told.shape))
-    value_poly = told[:, :value_rows].reshape(seq_count * per, P_SIZE, P_SIZE)[:heads]
-    small = told[:, value_rows:].reshape(seq_count * small_rows, LANES)
+    value_poly, small = told_all(value_own, summed[value_rows:], value_rows, small_rows)
     state_poly = chain(
         jnp.stack(
             [small[:N], small[N : 2 * N], jnp.pad(small[2 * N : 2 * N + H], ((0, N - H), (0, 0)))]
         )
     )
-    value_orth = apply_heads(value_update, value_poly)
+    value_orth = apply_heads(value_update, value_poly[:heads])
     state_orth = jnp.concatenate(
         [
             jnp.einsum("rup,upq->ruq", map_update, state_poly[:2], precision=highest).reshape(
@@ -419,27 +459,6 @@
     new_value_weight = value_weight - factor * value_orth
     new_state_weight = state_weight - factor * state_orth
 
-    vectors = small[2 * N + H :]
-    at = D // LANES
-    norm_gain_grad = vectors[:at].reshape(D)
-    other = swapped(vectors)
-    first = jnp.where(model_index == 0, vectors, other)
-    second = jnp.where(model_index == 0, other, vectors)
-    conv_rows = (K + 1) * (inner + 2 * N) // LANES
-    conv_first, conv_second = (
-        side[at : at + conv_rows].reshape(K + 1, inner + 2 * N) for side in (first, second)
-    )
-    conv_value_grad = jnp.concatenate([conv_first[:, :inner], conv_second[:, :inner]], 1)
-    conv_state_grad = conv_first[:, inner:]
-    at = at + conv_rows
-    gated_rows = inner // LANES
-    gated_gain_grad = jnp.concatenate(
-        [first[at : at + gated_rows].reshape(inner), second[at : at + gated_rows].reshape(inner)]
-    )
-    at = at + gated_rows
-    head_params_grad = jnp.concatenate(
-        [first[at : at + 3, :heads], second[at : at + 3, :heads]], 1
-    )
     new_norm_gain, new_norm_velocity = vector_step(norm_gain, norm_gain_grad, norm_gain_velocity)
     new_conv_value, new_conv_value_velocity = vector_step(
         conv_value, conv_value_grad, conv_value_velocity

time: 743 us -> 778 us (1.047)
  local copies, waits for them, and re-layouts: 41.6 us -> 69.3 us
  blocking collectives: 58.4 us -> 38.9 us
  waiting for transfers between devices: 377 us -> 394 us
    unnamed x4 -> x6, waiting for transfers between devices: 0.07 us -> 245 us
    reduce_scatter x2 -> x0, waiting for transfers between devices: 204 us -> none  [the longest x1 108 us: body(): lax.psum_scatter(jnp.concatenate([dot_first(features, grad_gate), dot_fir...]
    dot_general x9 -> x13, matrix products: 23.1 us -> 45.7 us  [the longest x1 10.8 us: body(): raw = jnp.dot(features, mixed_full, precision=highest)]
    unnamed x226 -> x273, local copies, waits for them, and re-layouts: 11.5 us -> 32.6 us
    all_to_all x2 -> x1, blocking collectives: 58.4 us -> 38.9 us  [exchange(): return lax.all_to_all(array, 'seq', 0, 0, tiled=True)]
    all_gather x1, waiting for transfers between devices: 40.2 us -> 26.5 us  [body(): lax.all_gather(jnp.concatenate([gate_weight, out_weight], 1), 'seq', axis...]
    dot_general x4 -> x2, matrix products: 20.2 us -> 11.5 us  [matmul(): return jnp.dot(left, right, precision=high)]
    dot_general x4 -> x3, matrix products: 15.2 us -> 6.56 us  [dot_first(): lax.dot_general(left, right, (((0,), (0,)), ((), ())), precision=high)]
  transfers between devices with their start and end apart: 18 -> 21, of which waited for: 13 -> 11; matrix products, arithmetic and copies ran while one was open for 17% -> 22% of each run, Pallas kernels for 2% -> 2%
where the time goes in v2:
time: 778 us; the launch traced here: 767 us
  waiting for transfers between devices  394 us (51%)
  matrix products  91.7 us (12%)
  other arithmetic  82.5 us (11%)
  local copies, waits for them, and re-layouts  69.3 us (9%)
  starting transfers between devices  49.1 us (6%)
  blocking collectives  38.9 us (5%)
  between operations  23.6 us (3%)
  Pallas kernels  18.1 us (2%)
    unnamed x6, waiting for transfers between devices  245 us
    all_gather x1, waiting for transfers between devices, body(): lax.all_gather(jnp.concatenate([value_weight, own_map, own_step], 1), 'se...  77.3 us
    all_to_all x7, waiting for transfers between devices, exchange(): return lax.all_to_all(array, 'seq', 0, 0, tiled=True)  43.6 us
    all_to_all x1, blocking collectives, exchange(): return lax.all_to_all(array, 'seq', 0, 0, tiled=True)  38.9 us
    all_to_all x7, starting transfers between devices, exchange(): return lax.all_to_all(array, 'seq', 0, 0, tiled=True)  38 us
    unnamed x273, local copies, waits for them, and re-layouts  32.6 us
    all_gather x1, waiting for transfers between devices, body(): lax.all_gather(jnp.concatenate([gate_weight, out_weight], 1), 'seq', axis...  26.5 us
    dot_general x3, matrix products, dot_last(): lax.dot_general(left, right, (((1,), (1,)), ((), ())), precision=high)  19.6 us
  transfers between devices with their start and end apart: 21, of which 11 were waited for; matrix products, arithmetic and copies ran while one was open for 22% of the time, Pallas kernels for 2%

profile of v2, /device:TPU:0, one launch (start us, length us, event | category | flops | bytes accessed | tf_op | source)
XLA Modules:
  0.0 767.3 jit_solution(1725965621020551780)
XLA Ops:
  11.9 4.9 collective-permute-start
  21.1 77.3 %all-gather.3.cloned.1.call-done = f32[1024,1168]{1,0:T(8,128)} async-done(((f32[64,1168]{1,0:T(8,128)}), f32[1024,1168]{1,0:T(8,128)}) %all-gather.3.cloned.1.call-update) | async-done | bytes 4784144 | tf_op jit(solution)/shard_map/all_gather | solution.py:227
  98.4 10.8 %fusion.55 = f32[256,1168]{0,1:T(8,128)S(1)} fusion(f32[1024,1168]{1,0:T(8,128)} %all-gather.3.cloned.1.call-done, f32[256,1024]{1,0:T(8,128)S(1)} %copy-done, f32[1024]{0:T(1024)S(1)} %copy-done.46, f32[256]{0:T(256)S(1)} %add_rsqrt_fusion), kind=kOutput, calls=%fused_computation.96 | convolution fusion | flops 3674734592 | bytes 7033856 | tf_op jit(solution)/shard_map/dot_general | solution.py:246
  118.0 5.5 fusion.37
  126.7 38.9 %all_to_all.40.part_ref = f32[16,72,128]{2,1,0:T(8,128)} all-to-all(f32[16,72,128]{2,1,0:T(8,128)S(1)} %pad_maximum_fusion.4), channel_id=1, replica_groups=mesh['seq'=16,'mp'=2] {'seq'}, dimensions={0} | all-to-all | bytes 1179648 | tf_op jit(solution)/shard_map/all_to_all | solution.py:45
  176.0 19.9 %all-to-all-done.1 = f32[16,64,128]{2,1,0:T(8,128)} async-done(((f32[16,64,128]{2,1,0:T(8,128)}), f32[16,64,128]{2,1,0:T(8,128)}, u32[]{:S(2)}, u32[]{:S(2)}) %all-to-all-start.1) | async-done | bytes 524320 | tf_op jit(solution)/shard_map/all_to_all | solution.py:45
  199.0 6.0 multiply_add_fusion.4
  205.1 26.5 %all-gather.5.cloned.1.call-done = f32[1024,2048]{1,0:T(8,128)} async-done(((f32[64,2048]{1,0:T(8,128)}), f32[1024,2048]{1,0:T(8,128)}) %all-gather.5.cloned.1.call-update) | async-done | bytes 8388624 | tf_op jit(solution)/shard_map/all_gather | solution.py:230
  231.6 5.8 fusion.12
  237.4 5.8 multiply_reduce_fusion.12
  267.7 13.1 %all-to-all-done.2.part_ref = f32[16,72,128]{2,1,0:T(8,128)} async-done(((f32[16,72,128]{2,1,0:T(8,128)}), f32[16,72,128]{2,1,0:T(8,128)}, u32[]{:S(2)}, u32[]{:S(2)}) %all-to-all-start.2) | async-done | bytes 589856 | tf_op jit(solution)/shard_map/all_to_all | solution.py:45
  287.1 8.0 %fusion.14 = (f32[16,256]{1,0:T(8,128)}, f32[16,256]{1,0:T(8,128)}, f32[256,256]{1,0:T(8,128)}) fusion(f32[256,256]{1,0:T(8,128)} %fusion.121, f32[16,256]{1,0:T(8,128)} %copy-done.79, pred[256,256]{1,0:T(8,128)(4,1)} %fusion.92, f32[256,16,64]{0,2,1:T(8,128)S(1)} %bitcast.188, f32[256,16,64]{0,2,1:T(8,128)} %bitcast.196, f32[256,16]{0,1:T(8,128)S(1)} %copy-done.50), kind=kOutput, calls=%fused_computation.15 | convolution fusion | flops 814931968 | bytes 2752512 | tf_op jit(solution)/shard_map/ihp,jhp->hij/dot_general | solution.py:322
  356.7 5.9 copy.417
  362.7 9.0 %copy.415 = f32[1024,2112]{1,0:T(8,128)} copy(f32[1024,2112]{0,1:T(8,128)} %maximum_maximum_fusion) | data formatting | bytes 17301504
  376.8 5.8 fusion.10
  382.6 7.0 convolution_add_fusion
  390.2 90.5 %reduce-scatter.9.cloned.1.call-done = f32[64,1248]{1,0:T(8,128)} async-done(((f32[1024,1248]{1,0:T(8,128)}), f32[64,1248]{1,0:T(8,128)}) %reduce-scatter.9.cloned.1.call-update) | async-done | bytes 319504
  489.5 6.9 all-to-all-start.6
  496.6 6.8 fusion.6
  507.1 9.0 %all-to-all-done.6 = f32[16,56,128]{2,1,0:T(8,128)} async-done(((f32[16,56,128]{2,1,0:T(8,128)}), f32[16,56,128]{2,1,0:T(8,128)}, u32[]{:S(2)}, u32[]{:S(2)}) %all-to-all-start.6) | async-done | bytes 458784 | tf_op jit(solution)/shard_map/all_to_all | solution.py:45
  528.3 154.4 %reduce-scatter.7.cloned.1.call-done = f32[64,2112]{1,0:T(8,128)} async-done(((f32[1024,2112]{1,0:T(8,128)}), f32[64,2112]{1,0:T(8,128)}) %reduce-scatter.7.cloned.1.call-update) | async-done | bytes 540688
  690.8 7.5 all-to-all-start.4
  722.4 5.5 all-to-all-start.5
  728.6 5.8 chain.5
  (511 shorter events, 207.1 us)
Async XLA Ops:
  7.2 91.2 %all-gather.3.cloned.1.call-start = ((), (), s32[]{:S(2)}) async-start(), calls=%async_computation.10 | async-start | bytes 5570560 | tf_op jit(solution)/shard_map/all_gather | solution.py:227
  10.9 220.7 %all-gather.5.cloned.1.call-start = ((), (), s32[]{:S(2)}) async-start(), calls=%async_computation.11 | async-start | bytes 8912896 | tf_op jit(solution)/shard_map/all_gather | solution.py:230
  11.9 8.4 %collective-permute-start = (f32[3]{0:T(128)S(1)}, f32[3]{0:T(128)S(1)}, u32[]{:S(2)}, u32[]{:S(2)}) collective-permute-start(f32[3]{0:T(128)S(1)} %slice.246), channel_id=1, source_target_pairs={{0,2},{2,4},{4,6},{6,8},{8,10},{10,12},{12,14},{14,16},{16,18},{18... | collective-permute-start | bytes 44 | tf_op jit(solution)/shard_map/ppermute | solution.py:33
  19.7 228.8 %copy-start.77 = (f32[256]{0:T(256)}, f32[256]{0:T(256)S(1)}, u32[]{:S(2)}) copy-start(f32[256]{0:T(256)S(1)} %add_rsqrt_fusion) | copy-start | bytes 3076
  111.5 6.2 collective-permute-start.1
  123.5 1.4 collective-permute-start.2
  167.5 28.4 %all-to-all-start.1 = ((f32[16,64,128]{2,1,0:T(8,128)}), f32[16,64,128]{2,1,0:T(8,128)}, u32[]{:S(2)}, u32[]{:S(2)}) async-start(f32[16,64,128]{2,1,0:T(8,128)} %carry.2), calls=%async_computation.1 | async-start | bytes 1048576 | tf_op jit(solution)/shard_map/all_to_all | solution.py:45
  243.2 1.2 collective-permute-start.3
  259.4 21.4 %all-to-all-start.2 = ((f32[16,72,128]{2,1,0:T(8,128)}), f32[16,72,128]{2,1,0:T(8,128)}, u32[]{:S(2)}, u32[]{:S(2)}) async-start(f32[16,72,128]{2,1,0:T(8,128)} %pad_maximum_fusion.3), calls=%async_computation.2 | async-start | bytes 1179648 | tf_op jit(solution)/shard_map/all_to_all | solution.py:45
  282.8 22.8 %all-to-all-start.3 = ((f32[16,64,128]{2,1,0:T(8,128)}), f32[16,64,128]{2,1,0:T(8,128)}, u32[]{:S(2)}, u32[]{:S(2)}) async-start(f32[16,64,128]{2,1,0:T(8,128)} %carry.3), calls=%async_computation.3 | async-start | bytes 1048576 | tf_op jit(solution)/shard_map/all_to_all | solution.py:45
  287.1 193.7 %reduce-scatter.9.cloned.1.call-start = ((), (), s32[]{:S(2)}) async-start(), calls=%async_computation.13 | async-start | bytes 5570560
  310.3 21.8 %collective-permute-start.5 = (f32[256,128]{0,1:T(8,128)}, f32[256,128]{0,1:T(8,128)}, u32[]{:S(2)}, u32[]{:S(2)}) collective-permute-start(f32[256,128]{0,1:T(8,128)} %get-tuple-element.361), channel_id=1, source_target_pairs={{0,1},{1,0},{2,3},{3,2},{4,5},{5,4},{6,7},{7,6},{8,9},{9,8},{10,11... | collective-permute-start | bytes 393224 | tf_op jit(solution)/shard_map/ppermute | solution.py:37
  342.5 5.7 collective-permute-start.6
  362.6 320.1 %reduce-scatter.7.cloned.1.call-start = ((), (), s32[]{:S(2)}) async-start(), calls=%async_computation.12 | async-start | bytes 9469952
  389.6 115.2 %collective-permute-start.7 = (f32[256,1024]{1,0:T(8,128)S(1)}, f32[256,1024]{1,0:T(8,128)}, u32[]{:S(2)}, u32[]{:S(2)}) collective-permute-start(f32[256,1024]{1,0:T(8,128)S(1)} %convolution_add_fusion), channel_id=1, source_target_pairs={{0,1},{1,0},{2,3},{3,2},{4,5},{5,4},{6,7},{7,6},{8,9},{9,8},{10,11... | collective-permute-start | bytes 3145736 | tf_op jit(solution)/shard_map/ppermute | solution.py:37
  482.3 4.0 collective-permute-start.8
  489.5 26.5 %all-to-all-start.6 = ((f32[16,56,128]{2,1,0:T(8,128)}), f32[16,56,128]{2,1,0:T(8,128)}, u32[]{:S(2)}, u32[]{:S(2)}) async-start(f32[16,56,128]{2,1,0:T(8,128)} %pad_maximum_fusion.7), calls=%async_computation.6 | async-start | bytes 917504 | tf_op jit(solution)/shard_map/all_to_all | solution.py:45
  503.4 200.1 %collective-permute-start.4 = (f32[256,1024]{1,0:T(8,128)}, f32[256,1024]{1,0:T(8,128)}, u32[]{:S(2)}, u32[]{:S(2)}) collective-permute-start(f32[256,1024]{1,0:T(8,128)} %fusion.6), channel_id=1, source_target_pairs={{0,1},{1,0},{2,3},{3,2},{4,5},{5,4},{6,7},{7,6},{8,9},{9,8},{10,11... | collective-permute-start | bytes 3145736 | tf_op jit(solution)/shard_map/ppermute | solution.py:37
  523.4 167.4 %all-to-all-start.7 = ((f32[16,56,128]{2,1,0:T(8,128)}), f32[16,56,128]{2,1,0:T(8,128)}, u32[]{:S(2)}, u32[]{:S(2)}) async-start(f32[16,56,128]{2,1,0:T(8,128)} %broadcast_in_dim.29), calls=%async_computation.7 | async-start | bytes 917504 | tf_op jit(solution)/shard_map/all_to_all | solution.py:45
  528.2 156.4 %copy-start.24 = (f32[64,1024]{0,1:T(8,128)S(1)}, f32[64,1024]{0,1:T(8,128)}, u32[]{:S(2)}) copy-start(f32[64,1024]{0,1:T(8,128)} %copy.365) | copy-start | bytes 786436
  528.2 156.4 %copy-start.25 = (f32[64,1024]{0,1:T(8,128)S(1)}, f32[64,1024]{0,1:T(8,128)}, u32[]{:S(2)}) copy-start(f32[64,1024]{0,1:T(8,128)} %copy.366) | copy-start | bytes 786436
  690.8 23.6 %all-to-all-start.4 = ((f32[16,72,128]{2,1,0:T(8,128)}), f32[16,72,128]{2,1,0:T(8,128)}, u32[]{:S(2)}, u32[]{:S(2)}) async-start(f32[16,72,128]{2,1,0:T(8,128)} %pad_maximum_fusion.5), calls=%async_computation.4 | async-start | bytes 1179648 | tf_op jit(solution)/shard_map/all_to_all | solution.py:45
  722.4 22.4 %all-to-all-start.5 = ((f32[16,72,128]{2,1,0:T(8,128)}), f32[16,72,128]{2,1,0:T(8,128)S(1)}, u32[]{:S(2)}, u32[]{:S(2)}) async-start(f32[16,72,128]{2,1,0:T(8,128)} %broadcast_in_dim.28), calls=%async_computation.5 | async-start | bytes 1179648 | tf_op jit(solution)/shard_map/all_to_all | solution.py:45
  746.3 5.4 collective-permute-start.9
  (125 other events, 1929.7 us)
Sparse Core Ops, SparseCore 0:
  11.4 87.0 all-gather.2
  101.8 129.7 all-gather.4
  362.7 117.9 reduce-scatter.8
  482.9 199.7 reduce-scatter.6
